TPU v7x, 256 devices: a whole 4x4x8 slice. The times are simulated.
256 devices in a mesh: row: 64 (over y, z, core), col: 4 (over x).
Axes of the slice: x: 4, y: 4, z: 8, core: 2. Of those that a mesh axis runs over, the one named last changes fastest.
Arguments:
- fractions_source: float32 [12, 4096, 4096], P('col', 'row'), may hold values from 0 to 1, as said below
- x_source_edges: int32 [4097], replicated, may hold values from 0 to 196608, as said below
- x_target_edges: int32 [3073], replicated, may hold values from 0 to 196608, as said below
- y_source_edges: int32 [4097], replicated, may hold values from 0 to 196608, as said below
- y_target_edges: int32 [3073], replicated, may hold values from 0 to 196608, as said below
- conductivity_table: int32 [6], replicated, may hold values from 4 to 64
- capacity: float32 [6], replicated, may hold values from 0.5 to 4
- thermal_source_term: float32 [2, 3072, 3072], P(None, 'row', 'col'), may hold values from -40 to 40
Outputs:
- rezoned_occupancy_shares: float32 [12, 3072, 3072], P(None, 'row', 'col')
- thermal_iterate: float32 [2, 3072, 3072], P(None, 'row', 'col')
- remaining_defect: float32 [2, 3072, 3072], P(None, 'row', 'col')
Inputs may be any that keep to these rules, and one draw needn't show every extreme that they name: `fractions_source`: positive; for every z layer and source cell the 6 materials' fractions sum to one. `x_source_edges`: strictly increasing; every 64-th source edge along x coincides with every 48-th target edge along x, at multiples of 3072; the first edge is 0 and the last is the largest value. `x_target_edges`: strictly increasing; shares the walls of x_source_edges at every 48-th edge; the first edge is 0 and the last is the largest value. `y_source_edges`: strictly increasing; every 64-th source edge along y coincides with every 48-th target edge along y, at multiples of 3072; the first edge is 0 and the last is the largest value. `y_target_edges`: strictly increasing; shares the walls of y_source_edges at every 48-th edge; the first edge is 0 and the last is the largest value.
All inputs are finite; a program needn't handle non-finite values.
Results may differ from a plain program's by a relative error of at most 0.0003.
Values sent between devices are 32-bit elements; how exact they have to be, the bound alone decides.
A program may use at most 64 MiB of HBM per device.

v0:
```python
import jax
import jax.numpy as jnp
from jax import lax
from jax.sharding import PartitionSpec as P

M = 6
SBLK = 64
TBLK = 48
ITERS = 3


def extended(cells, sides, width):
    for axis, dim in sides:
        count = lax.axis_size(axis)
        ends = count - 1
        head = lax.slice_in_dim(cells, 0, width, axis=dim)
        tail = lax.slice_in_dim(cells, cells.shape[dim] - width, cells.shape[dim], axis=dim)
        cells = jnp.concatenate(
            [
                lax.ppermute(tail, axis, [(i, (i + 1) % count) for i in range(ends)]),
                cells,
                lax.ppermute(head, axis, [((i + 1) % count, i) for i in range(ends)]),
            ],
            axis=dim,
        )
    return cells


def margin_blocks(source_edges, target_mesh_edges, source_block, target_block):
    block_list = (source_edges.shape[0] - 1) // source_block
    src_lo = source_edges[:-1].reshape(block_list, 1, source_block)
    src_hi = source_edges[1:].reshape(block_list, 1, source_block)
    tgt_lo = target_mesh_edges[:-1].reshape(block_list, target_block, 1)
    tgt_hi = target_mesh_edges[1:].reshape(block_list, target_block, 1)
    shared = jnp.maximum(jnp.minimum(src_hi, tgt_hi) - jnp.maximum(src_lo, tgt_lo), 0)
    return shared.astype(jnp.float32) / (tgt_hi - tgt_lo).astype(jnp.float32)


def face_weights(padded_array):
    center = padded_array[1:-1, 1:-1, 1:-1]
    neighbours = (
        padded_array[2:, 1:-1, 1:-1],
        padded_array[:-2, 1:-1, 1:-1],
        padded_array[1:-1, 2:, 1:-1],
        padded_array[1:-1, :-2, 1:-1],
        padded_array[1:-1, 1:-1, 2:],
        padded_array[1:-1, 1:-1, :-2],
    )
    return tuple((2.0 * center * beside / (center + beside) for beside in neighbours))


def stencil(padded_field, face_list, cell_capacity):
    center = padded_field[1:-1, 1:-1, 1:-1]
    neighbours = (
        padded_field[2:, 1:-1, 1:-1],
        padded_field[:-2, 1:-1, 1:-1],
        padded_field[1:-1, 2:, 1:-1],
        padded_field[1:-1, :-2, 1:-1],
        padded_field[1:-1, 1:-1, 2:],
        padded_field[1:-1, 1:-1, :-2],
    )
    result = cell_capacity * center
    for weight, beside in zip(face_list, neighbours):
        result = result + weight * (center - beside)
    return result


def squares(remaining_defect):
    return lax.psum(jnp.sum(remaining_defect * remaining_defect), ("row", "col"))


def per_device(
    fractions_source,
    x_source_edges,
    x_target_edges,
    y_source_edges,
    y_target_edges,
    conductivity_table,
    capacity,
    thermal_source_term,
):
    weight_x = margin_blocks(x_source_edges, x_target_edges, SBLK, TBLK)
    vertical_factor = margin_blocks(y_source_edges, y_target_edges, SBLK, TBLK)
    my_pairs = fractions_source.shape[0]
    block_list = vertical_factor.shape[0]
    source_grid = fractions_source.reshape(my_pairs, SBLK, block_list, SBLK)
    along_y = jnp.einsum(
        "psbu,bvu->psbv", source_grid, vertical_factor, precision=lax.Precision.HIGHEST
    )
    along_y = along_y.reshape(my_pairs, SBLK, block_list * TBLK)
    regrouped = lax.all_to_all(along_y, "row", split_axis=2, concat_axis=1, tiled=True)
    column_count = regrouped.reshape(my_pairs, block_list, SBLK, TBLK)
    rezoned = jnp.einsum("pasv,ats->pvat", column_count, weight_x, precision=lax.Precision.HIGHEST)
    rezoned = rezoned.reshape(my_pairs, TBLK, block_list * TBLK)
    rezoned_occupancy_shares = lax.all_to_all(
        rezoned, "col", split_axis=2, concat_axis=0, tiled=True
    )
    zlayers = thermal_source_term.shape[0]
    stacked = rezoned_occupancy_shares.reshape(
        zlayers, M, rezoned_occupancy_shares.shape[1], rezoned_occupancy_shares.shape[2]
    )
    substance_diffusivity = conductivity_table.astype(jnp.float32) / 16.0
    inverse = jnp.sum(stacked / substance_diffusivity[None, :, None, None], axis=1)
    cell_k = 1.0 / inverse
    cell_capacity = jnp.sum(stacked * capacity[None, :, None, None], axis=1)
    padded_k = extended(cell_k, (("row", 1), ("col", 2)), 1)
    padded_k = jnp.pad(padded_k, ((1, 1), (0, 0), (0, 0)))
    face_list = face_weights(padded_k)
    thermal_iterate = jnp.zeros_like(thermal_source_term)
    remaining_defect = thermal_source_term
    conjugate_update_vector = thermal_source_term
    norm_now = squares(remaining_defect)
    for iteration in range(ITERS):
        padded_field = extended(conjugate_update_vector, (("row", 1), ("col", 2)), 1)
        padded_field = jnp.pad(padded_field, ((1, 1), (0, 0), (0, 0)))
        applied = stencil(padded_field, face_list, cell_capacity)
        line_minimizer_alpha = norm_now / lax.psum(
            jnp.sum(conjugate_update_vector * applied), ("row", "col")
        )
        thermal_iterate = thermal_iterate + line_minimizer_alpha * conjugate_update_vector
        remaining_defect = remaining_defect - line_minimizer_alpha * applied
        norm_next = squares(remaining_defect)
        conjugate_update_vector = remaining_defect + norm_next / norm_now * conjugate_update_vector
        norm_now = norm_next
    return (rezoned_occupancy_shares, thermal_iterate, remaining_defect)


def solution(mesh):
    placed = (P("col", "row", None), P(), P(), P(), P(), P(), P(), P(None, "row", "col"))
    return jax.shard_map(
        per_device,
        mesh=mesh,
        in_specs=placed,
        out_specs=(P(None, "row", "col"), P(None, "row", "col"), P(None, "row", "col")),
        check_vma=False,
    )
```

profile of v0, /device:TPU:1, one launch (start us, length us, event | category | flops | bytes accessed | tf_op | source)
XLA Modules:
  0.0 646.9 jit_solution(14639724747322265408)
XLA Ops:
  2.7 6.1 reshape.75
  8.8 16.5 %fusion.5 = f32[3,64,64,48]{1,3,0,2:T(8,128)S(1)} fusion(f32[3,64,64,64]{3,2,1,0:T(8,128)} %reshape.75, f32[64,48]{1,0:T(8,128)S(1)} %subtract_convert_fusion, s32[64,48]{1,0:T(8,128)S(1)} %max.48, s32[64,64]{1,0:T(8,128)S(1)} %max.46, s32[64,48]{1,0:T(8,128)S(1)} %min.41, s32[64,64]{1,0:T(8,128)S(1)} %min.39), kind=kOutput, calls=%fused_computation.5 | convolution fusion | flops 454164480 | bytes 5574656 | tf_op jit(solution)/shard_map/psbu,bvu->psbv/dot_general | solution.py:87
  25.3 5.2 copy.82
  30.6 8.5 %reshape.80 = f32[64,1,9216]{2,1,0:T(1,128)} reshape(f32[3072,3,64]{2,1,0:T(4,128)} %bitcast.45) | data formatting | bytes 4718592
  39.1 13.6 %all-to-all-start = ((f32[64,1,9216]{2,1,0:T(1,128)}), f32[64,1,9216]{2,1,0:T(1,128)S(1)}, u32[]{:S(2)}, u32[]{:S(2)}) async-start(f32[64,1,9216]{2,1,0:T(1,128)} %reshape.80), calls=%async_computation | async-start | bytes 4718592 | tf_op jit(solution)/shard_map/all_to_all | solution.py:91
  53.1 56.0 %all-to-all-done = f32[64,1,9216]{2,1,0:T(1,128)S(1)} async-done(((f32[64,1,9216]{2,1,0:T(1,128)}), f32[64,1,9216]{2,1,0:T(1,128)S(1)}, u32[]{:S(2)}, u32[]{:S(2)}) %all-to-all-start) | async-done | bytes 2359328 | tf_op jit(solution)/shard_map/all_to_all | solution.py:91
  109.7 8.3 %reduce.4 = f32[64,9216]{1,0:T(8,128)} reduce(f32[64,1,9216]{2,1,0:T(1,128)S(1)} %all-to-all-done, f32[]{:T(128)} %broadcast.163), dimensions={1}, to_apply=%all_to_all.24.reduce_sub_computation | reduce | bytes 4718596 | tf_op jit(solution)/shard_map/all_to_all | solution.py:91
  118.0 6.6 %reshape.81 = f32[3072,3,64]{2,1,0:T(4,128)} reshape(f32[64,9216]{1,0:T(8,128)} %reduce.4) | data formatting | bytes 4718592
  124.6 14.4 %fusion.8 = f32[3,48,64,48]{1,3,0,2:T(8,128)S(1)} fusion(f32[3,64,64,48]{1,0,3,2:T(4,128)} %bitcast.47, f32[64,48]{1,0:T(8,128)S(1)} %subtract_convert_fusion.1, s32[64,48]{1,0:T(8,128)S(1)} %max.42, s32[64,64]{1,0:T(8,128)S(1)} %max.40, s32[64,48]{1,0:T(8,128)S(1)} %min.36, s32[64,64]{1,0:T(8,128)S(1)} %min.34), kind=kOutput, calls=%fused_computation.6 | convolution fusion | flops 340918272 | bytes 4198400 | tf_op jit(solution)/shard_map/pasv,ats->pvat/dot_general | solution.py:93
  139.0 5.2 copy.85
  144.3 8.1 %reshape.82 = f32[4,1,110592]{2,1,0:T(1,128)} reshape(f32[3072,3,48]{2,1,0:T(4,128)} %bitcast.46) | data formatting | bytes 3538944
  152.4 4.2 all-to-all-start.1
  156.5 2.5 collective-permute-start.4
  161.4 17.5 %all-to-all-done.1 = f32[4,1,110592]{2,1,0:T(1,128)S(1)} async-done(((f32[4,1,110592]{2,1,0:T(1,128)}), f32[4,1,110592]{2,1,0:T(1,128)S(1)}, u32[]{:S(2)}, u32[]{:S(2)}) %all-to-all-start.1) | async-done | bytes 1769504 | tf_op jit(solution)/shard_map/all_to_all | solution.py:95
  178.9 7.0 %reduce.5 = f32[4,110592]{1,0:T(4,128)} reduce(f32[4,1,110592]{2,1,0:T(1,128)S(1)} %all-to-all-done.1, f32[]{:T(128)} %broadcast.163), dimensions={1}, to_apply=%all_to_all.27.reduce_sub_computation | reduce | bytes 3538948 | tf_op jit(solution)/shard_map/all_to_all | solution.py:95
  185.9 9.1 %reshape.83 = f32[3072,3,48]{2,1,0:T(4,128)} reshape(f32[4,110592]{1,0:T(4,128)} %reduce.5) | data formatting | bytes 3538944
  195.0 5.2 copy.86
  203.4 3.5 collective-permute-start
  213.2 4.0 collective-permute-start.2
  223.3 2.5 multiply_reduce_fusion.4
  225.7 75.7 %all-reduce.4 = (f32[]{:T(128)}, f32[]{:T(128)}) all-reduce(f32[]{:T(128)} %get-tuple-element.9, f32[]{:T(128)} %get-tuple-element.8), channel_id=1, replica_groups=mesh['row'=64,'col'=4] {'row','col'}, use_global_device_ids=true, to_apply=%region_1.0 | all-reduce | flops 2 | bytes 16 | tf_op jit(solution)/shard_map/psum | solution.py:69
  303.4 73.2 %psum.44 = f32[]{:T(128)} all-reduce(f32[]{:T(128)} %multiply_reduce_fusion.3), channel_id=1, replica_groups=mesh['row'=64,'col'=4] {'row','col'}, use_global_device_ids=true, to_apply=%region_9.10 | all-reduce | flops 1 | bytes 8 | tf_op jit(solution)/shard_map/psum | solution.py:69
  378.1 3.4 collective-permute-start.8
  383.4 3.0 collective-permute-done.9
  386.5 2.5 collective-permute-start.10
  390.3 3.6 collective-permute-done.11
  395.7 75.6 %psum.45 = f32[]{:T(128)} all-reduce(f32[]{:T(128)} %get-tuple-element.16), channel_id=1, replica_groups=mesh['row'=64,'col'=4] {'row','col'}, use_global_device_ids=true, to_apply=%region_11.12 | all-reduce | flops 1 | bytes 8 | tf_op jit(solution)/shard_map/psum | solution.py:117
  473.4 72.6 %psum.46 = f32[]{:T(128)} all-reduce(f32[]{:T(128)} %get-tuple-element.14), channel_id=1, replica_groups=mesh['row'=64,'col'=4] {'row','col'}, use_global_device_ids=true, to_apply=%region_13.14 | all-reduce | flops 1 | bytes 8 | tf_op jit(solution)/shard_map/psum | solution.py:69
  547.4 4.2 collective-permute-start.12
  553.5 3.0 collective-permute-done.13
  560.3 6.2 copy.73
  568.2 76.3 %psum.47 = f32[]{:T(128)} all-reduce(f32[]{:T(128)} %get-tuple-element.12), channel_id=1, replica_groups=mesh['row'=64,'col'=4] {'row','col'}, use_global_device_ids=true, to_apply=%region_15.16 | all-reduce | flops 1 | bytes 8 | tf_op jit(solution)/shard_map/psum | solution.py:117
  (92 shorter events, 35.5 us)
Async XLA Ops:
  39.1 13.6 %copy-start.8 = (s32[3073]{0:T(1024)S(1)}, s32[3073]{0:T(1024)}, u32[]{:S(2)}) copy-start(s32[3073]{0:T(1024)} %param.10) | copy-start | bytes 36880
  39.1 13.8 %copy-start.7 = (s32[4097]{0:T(1024)S(1)}, s32[4097]{0:T(1024)}, u32[]{:S(2)}) copy-start(s32[4097]{0:T(1024)} %param.9) | copy-start | bytes 49168
  39.1 70.1 %all-to-all-start = ((f32[64,1,9216]{2,1,0:T(1,128)}), f32[64,1,9216]{2,1,0:T(1,128)S(1)}, u32[]{:S(2)}, u32[]{:S(2)}) async-start(f32[64,1,9216]{2,1,0:T(1,128)} %reshape.80), calls=%async_computation | async-start | bytes 4718592 | tf_op jit(solution)/shard_map/all_to_all | solution.py:91
  152.4 4.2 copy-start
  152.4 8.6 %copy-start.9 = (s32[6]{0:T(128)S(1)}, s32[6]{0:T(128)}, u32[]{:S(2)}) copy-start(s32[6]{0:T(128)} %param.13) | copy-start | bytes 76
  152.4 8.8 %copy-start.10 = (f32[6]{0:T(128)S(1)}, f32[6]{0:T(128)}, u32[]{:S(2)}) copy-start(f32[6]{0:T(128)} %param.14) | copy-start | bytes 76
  152.4 26.5 %all-to-all-start.1 = ((f32[4,1,110592]{2,1,0:T(1,128)}), f32[4,1,110592]{2,1,0:T(1,128)S(1)}, u32[]{:S(2)}, u32[]{:S(2)}) async-start(f32[4,1,110592]{2,1,0:T(1,128)} %reshape.82), calls=%async_computation.1 | async-start | bytes 3538944 | tf_op jit(solution)/shard_map/all_to_all | solution.py:95
  156.5 52.3 %collective-permute-start.4 = (f32[2,1,768]{2,1,0:T(1,128)S(1)}, f32[2,1,768]{2,1,0:T(1,128)S(1)}, u32[]{:S(2)}, u32[]{:S(2)}) collective-permute-start(f32[2,1,768]{2,1,0:T(1,128)S(1)} %get-tuple-element.33), channel_id=1, source_target_pairs={{0,4},{4,8},{8,12},{12,16},{16,20},{20,24},{24,28},{28,32},{32,36}... | collective-permute-start | bytes 18440 | tf_op jit(solution)/shard_map/ppermute | solution.py:20
  159.0 49.8 %collective-permute-start.5 = (f32[2,1,768]{2,1,0:T(1,128)S(1)}, f32[2,1,768]{2,1,0:T(1,128)S(1)}, u32[]{:S(2)}, u32[]{:S(2)}) collective-permute-start(f32[2,1,768]{2,1,0:T(1,128)S(1)} %get-tuple-element.34), channel_id=1, source_target_pairs={{4,0},{8,4},{12,8},{16,12},{20,16},{24,20},{28,24},{32,28},{36,32}... | collective-permute-start | bytes 18440 | tf_op jit(solution)/shard_map/ppermute | solution.py:22
  202.4 17.1 %copy-start.1 = (f32[4,48,768]{2,0,1:T(4,128)S(1)}, f32[4,48,768]{2,0,1:T(4,128)}, u32[]{:S(2)}) copy-start(f32[4,48,768]{2,0,1:T(4,128)} %get-tuple-element.7) | copy-start | bytes 1769476
  203.4 9.1 %collective-permute-start = (f32[2,1,768]{2,1,0:T(1,128)S(1)}, f32[2,1,768]{2,1,0:T(1,128)S(1)}, u32[]{:S(2)}, u32[]{:S(2)}) collective-permute-start(f32[2,1,768]{2,1,0:T(1,128)S(1)} %get-tuple-element.31), channel_id=1, source_target_pairs={{0,4},{4,8},{8,12},{12,16},{16,20},{20,24},{24,28},{28,32},{32,36}... | collective-permute-start | bytes 18440 | tf_op jit(solution)/shard_map/ppermute | solution.py:20
  206.9 5.6 collective-permute-start.1
  208.9 9.7 %copy-start.5 = (f32[2,1,768]{2,1,0:T(1,128)}, f32[2,1,768]{2,1,0:T(1,128)S(1)}, u32[]{:S(2)}) copy-start(f32[2,1,768]{2,1,0:T(1,128)S(1)} %collective-permute-done.4) | copy-start | bytes 18436
  208.9 9.7 %copy-start.6 = (f32[2,1,768]{2,1,0:T(1,128)}, f32[2,1,768]{2,1,0:T(1,128)S(1)}, u32[]{:S(2)}) copy-start(f32[2,1,768]{2,1,0:T(1,128)S(1)} %collective-permute-done.5) | copy-start | bytes 18436
  209.0 9.5 %collective-permute-start.6 = (f32[2,50,1]{2,1,0:T(8,128)S(1)}, f32[2,50,1]{2,1,0:T(8,128)S(1)}, u32[]{:S(2)}, u32[]{:S(2)}) collective-permute-start(f32[2,50,1]{2,1,0:T(8,128)S(1)} %get-tuple-element.26), channel_id=1, source_target_pairs={{0,1},{1,2},{2,3},{4,5},{5,6},{6,7},{8,9},{9,10},{10,11},{12,13},{... | collective-permute-start | bytes 1208 | tf_op jit(solution)/shard_map/ppermute | solution.py:20
  211.2 7.4 %collective-permute-start.7 = (f32[2,50,1]{2,1,0:T(8,128)S(1)}, f32[2,50,1]{2,1,0:T(8,128)S(1)}, u32[]{:S(2)}, u32[]{:S(2)}) collective-permute-start(f32[2,50,1]{2,1,0:T(8,128)S(1)} %get-tuple-element.25), channel_id=1, source_target_pairs={{1,0},{2,1},{3,2},{5,4},{6,5},{7,6},{9,8},{10,9},{11,10},{13,12},{... | collective-permute-start | bytes 1208 | tf_op jit(solution)/shard_map/ppermute | solution.py:22
  212.5 10.5 %copy-start.3 = (f32[2,1,768]{2,1,0:T(1,128)}, f32[2,1,768]{2,1,0:T(1,128)S(1)}, u32[]{:S(2)}) copy-start(f32[2,1,768]{2,1,0:T(1,128)S(1)} %collective-permute-done.1) | copy-start | bytes 18436
  213.2 7.7 %collective-permute-start.2 = (f32[2,50,1]{2,1,0:T(8,128)}, f32[2,50,1]{2,1,0:T(8,128)S(1)}, u32[]{:S(2)}, u32[]{:S(2)}) collective-permute-start(f32[2,50,1]{2,1,0:T(8,128)} %get-tuple-element.24), channel_id=1, source_target_pairs={{0,1},{1,2},{2,3},{4,5},{5,6},{6,7},{8,9},{9,10},{10,11},{12,13},{... | collective-permute-start | bytes 1208 | tf_op jit(solution)/shard_map/ppermute | solution.py:20
  217.2 5.8 collective-permute-start.3
  218.6 4.5 copy-start.2
  225.7 168.4 %copy-start.4 = (f32[2,1,768]{2,1,0:T(1,128)S(1)}, f32[2,1,768]{2,1,0:T(1,128)}, u32[]{:S(2)}) copy-start(f32[2,1,768]{2,1,0:T(1,128)} %copy-done.3) | copy-start | bytes 18436
  378.1 5.3 collective-permute-start.8
  381.5 4.9 collective-permute-start.9
  386.5 3.8 collective-permute-start.10
  389.0 4.9 collective-permute-start.11
  547.4 6.2 collective-permute-start.12
  551.6 4.9 collective-permute-start.13
  556.6 9.8 %collective-permute-start.14 = (f32[2,50,1]{2,1,0:T(8,128)S(1)}, f32[2,50,1]{2,1,0:T(8,128)S(1)}, u32[]{:S(2)}, u32[]{:S(2)}) collective-permute-start(f32[2,50,1]{2,1,0:T(8,128)S(1)} %get-tuple-element.20), channel_id=1, source_target_pairs={{0,1},{1,2},{2,3},{4,5},{5,6},{6,7},{8,9},{9,10},{10,11},{12,13},{... | collective-permute-start | bytes 1208 | tf_op jit(solution)/shard_map/ppermute | solution.py:20
  559.0 7.5 %collective-permute-start.15 = (f32[2,50,1]{2,1,0:T(8,128)S(1)}, f32[2,50,1]{2,1,0:T(8,128)S(1)}, u32[]{:S(2)}, u32[]{:S(2)}) collective-permute-start(f32[2,50,1]{2,1,0:T(8,128)S(1)} %get-tuple-element.19), channel_id=1, source_target_pairs={{1,0},{2,1},{3,2},{5,4},{6,5},{7,6},{9,8},{10,9},{11,10},{13,12},{... | collective-permute-start | bytes 1208 | tf_op jit(solution)/shard_map/ppermute | solution.py:22
where the time goes:
time: 655 us; the launch traced here: 647 us
  blocking collectives  373 us (57%)
  waiting for transfers between devices  85.3 us (13%)
  local copies, waits for them, and re-layouts  64.6 us (10%)
  starting transfers between devices  55.2 us (8%)
  matrix products  30.9 us (5%)
  other arithmetic  29.4 us (4%)
  between operations  8.01 us (1%)
    psum x3, blocking collectives, squares(): lax.psum(jnp.sum(remaining_defect * remaining_defect), ('row', 'col'))  222 us
    psum x2, blocking collectives, per_device(): lax.psum(jnp.sum(conjugate_update_vector * applied), ('row', 'col'))  152 us
    all_to_all x1, waiting for transfers between devices, per_device(): lax.all_to_all(along_y, 'row', split_axis=2, concat_axis=1, tiled=True)  56 us
    unnamed x26, local copies, waits for them, and re-layouts  32.4 us
    ppermute x8, starting transfers between devices, extended(): lax.ppermute(tail, axis, [(i, (i + 1) % count) for i in range(ends)])  24.6 us
    all_to_all x1, waiting for transfers between devices, per_device(): lax.all_to_all(rezoned, 'col', split_axis=2, concat_axis=0, tiled=True)  17.5 us
    dot_general x1, matrix products, per_device(): jnp.einsum('psbu,bvu->psbv', source_grid, vertical_factor, precision=lax....  16.5 us
    dot_general x1, matrix products, per_device(): jnp.einsum('pasv,ats->pvat', column_count, weight_x, precision=lax.Precis...  14.4 us
  transfers between devices with their start and end apart: 18, of which 6 were waited for; matrix products, arithmetic and copies ran while one was open for 5% of the time, Pallas kernels for 0%

commit v1 on v0

v1 whole, which is shorter than its diff:
```python
import jax
import jax.numpy as jnp
from jax import lax
from jax.experimental import pallas as pl
from jax.experimental.pallas import tpu as pltpu
from jax.sharding import PartitionSpec as P

M = 6
TB = 48
NQ = 32
LAG_FORWARD = 6
LAG_MERGE = 12
MESH = pl.DeviceIdType.MESH
F32 = jnp.float32
BF16 = jnp.bfloat16
VM = pltpu.VMEM
DMA = pltpu.SemaphoreType.DMA


def split(a):
    high = a.astype(BF16)
    return high, (a - high.astype(F32)).astype(BF16)


def product(ah, al, bh, bl, dims):
    def dot(p, q):
        return lax.dot_general(p, q, (dims, ((), ())), preferred_element_type=F32)

    return dot(ah, bh) + (dot(ah, bl) + dot(al, bh))


def offsets(k):
    g, s = k // 8, k % 2
    dz = jnp.where(s == 0, 4 - g, jnp.where(g == 0, 0, 4 + g))
    return (k // 2) % 4, dz


def lanes(shape):
    return lax.broadcasted_iota(jnp.int32, shape, len(shape) - 1)


def kernel(
    frac, src_rows, tgt_cols, param, b_ref, shares_out, x_out, r_out,
    fbuf, wxp, wah, wal, wbh, wbl, sbuf, rb1, rb2, R, bx, ix, v1, v2, v3, cc,
    fu, fd, fl, fr, fz, hs_row, hr_row, hs_col, hr_col, acc, tile_a, got_a, tile_b, got_b,
    fsem, ssem, rsem1, ssem2, rsem2, hs_sem, hr_sem, ts_sem, tr_sem, osem,
):
    r = lax.axis_index("row")
    c = lax.axis_index("col")
    core = r % 2
    chip = r // 2
    y, z = chip // 8, chip % 8
    half = c % 2

    def fetch(k):
        dy, dz = offsets(k)
        q = ((y + dy) % 4) * 8 + (z + dz) % 8
        return pltpu.make_async_copy(
            frac.at[:, :, pl.ds(pl.multiple_of(q * 128, 128), 128)], fbuf.at[k], fsem.at[k]
        )

    @pl.loop(0, NQ)
    def _(k):
        fetch(k).start()

    barrier = pltpu.get_barrier_semaphore()

    def greet(row, col):
        pl.semaphore_signal(barrier, inc=1, device_id=(row, col), device_id_type=MESH)

    @pl.loop(1, 64)
    def _(j):
        greet((r + j) % 64, c)

    @pl.loop(1, 4)
    def _(j):
        greet(r, (c + j) % 4)

    @pl.loop(0, 9)
    def _(j):
        greet((r + 16 * (1 + j // 3)) % 64, (c + 1 + j % 3) % 4)

    def pair_weights(low, high, cols):
        t_low, t_high = cols[:, 0:1], cols[:, 32:33]
        shared = jnp.maximum(jnp.minimum(high, t_high) - jnp.maximum(low, t_low), 0.0)
        return shared / (t_high - t_low)

    wxp[...] = pair_weights(
        src_rows[pl.ds(64 + chip, 1), :],
        src_rows[pl.ds(96 + chip, 1), :],
        pltpu.roll(tgt_cols[...], 64 - chip, 1),
    )
    wx = wxp[pl.ds(pl.multiple_of(TB * core, 8), TB), :]
    wx = pltpu.roll(wx, 64 * core, 1)
    wx64 = pltpu.roll(wx, 64, 1)
    wxp[0:TB, :] = wx64
    hi, lo = split(jnp.concatenate([wx, wx64], axis=0))
    wah[...] = hi
    wal[...] = lo
    third = wxp[pl.ds(pl.multiple_of(24 * half, 8), 24), :]
    hi, lo = split(jnp.concatenate([third, jnp.zeros((8, 128), F32)], axis=0))
    wbh[...] = hi
    wbl[...] = lo

    for zl in range(2):
        bx[zl, 8:56, :] = b_ref[zl]
    acc[...] = jnp.zeros_like(acc)

    def fold(a):
        out = a[:, 0:128]
        for i in range(1, 6):
            out = out + a[:, 128 * i : 128 * (i + 1)]
        return out

    def rows_of(a):
        return jnp.sum(a, axis=0, keepdims=True)

    lane8 = lanes((8, 768))
    row8 = lax.broadcasted_iota(jnp.int32, (8, 768), 0)
    square = jnp.zeros((8, 768), F32)
    rough = jnp.zeros((8, 768), F32)
    for g in range(6):
        a = [bx[zl, 8 + 8 * g : 16 + 8 * g, :] for zl in range(2)]
        d = a[0] - a[1]
        rough = rough + d * d
        for zl in range(2):
            square = square + a[zl] * a[zl]
            d = jnp.where(lane8 == 0, 0.0, a[zl] - pltpu.roll(a[zl], 1, 1))
            rough = rough + d * d
            if g > 0:
                d = a[zl] - bx[zl, 7 + 8 * g : 15 + 8 * g, :]
            else:
                d = jnp.where(row8 == 0, 0.0, a[zl] - pltpu.roll(a[zl], 1, 0))
            rough = rough + d * d
    tile_a[0, 0:1, :] = rows_of(fold(square))
    tile_a[0, 1:2, :] = rows_of(fold(rough))

    pl.semaphore_wait(barrier, 75)

    lane48 = lanes((TB, 128))

    def rim_copies(i):
        up, down = (r + 63) % 64, (r + 1) % 64
        left, right = (c + 3) % 4, (c + 1) % 4
        def copy(src, dst, d, peer):
            return pltpu.make_async_remote_copy(
                src_ref=src, dst_ref=dst, send_sem=hs_sem.at[i, d], recv_sem=hr_sem.at[i, d],
                device_id=peer, device_id_type=MESH,
            )
        return (
            copy(hs_row.at[i, 0], hr_row.at[i, 0], 0, (down, c)),
            copy(hs_row.at[i, 1], hr_row.at[i, 1], 1, (up, c)),
            copy(hs_col.at[i, 0], hr_col.at[i, 0], 2, (r, right)),
            copy(hs_col.at[i, 1], hr_col.at[i, 1], 3, (r, left)),
        )

    def rim_start(i, f):
        for zl in range(2):
            hs_row[i, 0, zl : zl + 1, :] = f[zl, 55:56, :]
            hs_row[i, 1, zl : zl + 1, :] = f[zl, 8:9, :]
        hs_col[i, 0] = jnp.where(
            lane48 == 127, f[0, 8:56, 640:768], pltpu.roll(f[1, 8:56, 640:768], 127, 1)
        )
        hs_col[i, 1] = jnp.where(lane48 == 0, f[0, 8:56, 0:128], pltpu.roll(f[1, 8:56, 0:128], 1, 1))
        for copy in rim_copies(i):
            copy.start()

    def rim_wait(i, f):
        for copy in rim_copies(i):
            copy.wait()
        for zl in range(2):
            f[zl, 7:8, :] = hr_row[i, 0, zl : zl + 1, :]
            f[zl, 56:57, :] = hr_row[i, 1, zl : zl + 1, :]

    rim_start(0, bx)

    spot_a = r % 16
    spot_b = y * 4 + c

    def sum_copy(i, stage, j):
        if stage == 0:
            peer = (16 * y + (spot_a + j) % 16, c)
            src, dst = tile_a.at[i], got_a.at[i, spot_a]
        else:
            other = (spot_b + j) % 16
            peer = (16 * (other // 4) + spot_a, other % 4)
            src, dst = tile_b.at[i], got_b.at[i, spot_b]
        return pltpu.make_async_remote_copy(
            src_ref=src, dst_ref=dst, send_sem=ts_sem.at[i, stage], recv_sem=tr_sem.at[i, stage],
            device_id=peer, device_id_type=MESH,
        )

    def sum_start(i, stage):
        @pl.loop(1, 16)
        def _(j):
            sum_copy(i, stage, j).start()

    def sum_wait(i, stage):
        got = got_a if stage == 0 else got_b
        tile = tile_a if stage == 0 else tile_b
        spot = spot_a if stage == 0 else spot_b
        got[i, pl.ds(spot, 1)] = tile[i][None]
        landed = got.at[i, 0:15]
        pltpu.make_async_copy(landed, landed, tr_sem.at[i, stage]).wait()
        total = got[i, 0]
        for j in range(1, 16):
            total = total + got[i, j]
        return total

    def compute(k):
        dy, dz = offsets(k)
        q = ((y + dy) % 4) * 8 + (z + dz) % 8
        wy = pair_weights(
            src_rows[pl.ds(q, 1), :], src_rows[pl.ds(32 + q, 1), :],
            pltpu.roll(tgt_cols[...], (128 - q) % 128, 1),
        )
        wyh, wyl = split(wy)
        fetch(k).wait()
        f = fbuf[k]
        for p in range(3):
            acc[p] = acc[p] + jnp.sum(f[p].reshape(8, 8, 128), axis=0)
        f = f.reshape(192, 128)
        fh, fo = split(f)
        nn = ((1,), (0,))
        g0 = product(wah[...], wal[...], fh[0:128], fo[0:128], nn)
        g1 = product(wbh[...], wbl[...], fh[64:192], fo[64:192], nn)
        gh, go = split(jnp.concatenate([g0, g1], axis=0))
        out = product(wyh, wyl, gh, go, ((1,), (1,)))
        sbuf[2 * k] = out[0:TB]
        sbuf[2 * k + 1] = out[TB : 2 * TB]

    def send(k):
        dy, dz = offsets(k)
        q = ((y + dy) % 4) * 8 + (z + dz) % 8
        for s in range(2):
            mine = jnp.logical_and(q == chip, core == s)

            @pl.when(mine)
            def _():
                pltpu.make_async_copy(
                    sbuf.at[2 * k + s], rb1.at[2 * k + core], rsem1.at[2 * k + core]
                ).start()

            @pl.when(jnp.logical_not(mine))
            def _():
                pltpu.make_async_remote_copy(
                    src_ref=sbuf.at[2 * k + s], dst_ref=rb1.at[2 * k + core],
                    send_sem=ssem, recv_sem=rsem1.at[2 * k + core],
                    device_id=(2 * q + s, c), device_id_type=MESH,
                ).start()

    def forward(k):
        dy, dz = offsets(k)
        to = (y - dy + 4) % 4
        zs = (z - dz + 8) % 8
        for s in range(2):
            got = rb1.at[2 * k + s]
            pltpu.make_async_copy(got, got, rsem1.at[2 * k + s]).wait()
            slot = c * 16 + zs * 2 + s

            @pl.when(to == c)
            def _():
                pltpu.make_async_copy(got, rb2.at[slot], rsem2.at[slot]).start()

            @pl.when(to != c)
            def _():
                pltpu.make_async_remote_copy(
                    src_ref=got, dst_ref=rb2.at[slot], send_sem=ssem2, recv_sem=rsem2.at[slot],
                    device_id=(r, to), device_id_type=MESH,
                ).start()

    def merge(k):
        dy, dz = offsets(k)
        zs = (z - dz + 8) % 8

        @pl.when((y - dy + 4) % 4 == c)
        def _():
            for cs in range(4):
                for s in range(2):
                    block = zs * 2 + s
                    slot = cs * 16 + block
                    got = rb2.at[slot]
                    pltpu.make_async_copy(got, got, rsem2.at[slot]).wait()
                    chunk = rb2[slot]
                    for p in range(3):
                        width = TB if p < 2 else 24
                        pos = TB * block + (24 * (cs % 2) if p == 2 else 0)
                        t0 = pos // 128
                        off = pos % 128
                        t1 = jnp.minimum(t0 + 1, 5)
                        turned = pltpu.roll(chunk, (off + 256 - TB * p) % 128, 1)
                        m = (cs // 2) * M + 3 * (cs % 2) + p
                        here = pl.ds(pl.multiple_of(t0 * 128, 128), 128)
                        inside = jnp.logical_and(lane48 >= off, lane48 < off + width)
                        R[m, :, here] = jnp.where(inside, turned, R[m, :, here])
                        there = pl.ds(pl.multiple_of(t1 * 128, 128), 128)
                        R[m, :, there] = jnp.where(lane48 < off + width - 128, turned, R[m, :, there])

    @pl.loop(0, NQ + LAG_MERGE)
    def _(it):
        @pl.when(it < NQ)
        def _():
            compute(it)

        @pl.when(jnp.logical_and(it >= 1, it <= NQ))
        def _():
            send(it - 1)

        @pl.when(it == NQ)
        def _():
            hf = half.astype(F32)
            for p in range(3):
                v = rows_of(acc[p])
                tile_a[0, 2 + p : 3 + p, :] = v * (1.0 - hf)
                tile_a[0, 5 + p : 6 + p, :] = v * hf
            sum_start(0, 0)

        @pl.when(it == NQ + 5)
        def _():
            tile_b[0] = sum_wait(0, 0)
            sum_start(0, 1)

        @pl.when(jnp.logical_and(it >= LAG_FORWARD, it < NQ + LAG_FORWARD))
        def _():
            forward(it - LAG_FORWARD)

        @pl.when(it >= LAG_MERGE)
        def _():
            merge(it - LAG_MERGE)

    for t in range(6):
        at = slice(128 * t, 128 * (t + 1))
        low = lax.rem(lanes((1, 128)) + 128 * t, TB) < 24
        for zl in range(2):
            m = [R[M * zl + i, :, at] for i in range(M)]
            rest = 1.0 - (m[0] + m[1] + m[3] + m[4])
            m[2], m[5] = jnp.where(low, m[2], rest - m[5]), jnp.where(low, rest - m[2], m[5])
            R[M * zl + 2, :, at] = m[2]
            R[M * zl + 5, :, at] = m[5]
            inverse = m[0] * param[0]
            heat = m[0] * param[M]
            for i in range(1, M):
                inverse = inverse + m[i] * param[i]
                heat = heat + m[i] * param[M + i]
            ix[zl, 8:56, at] = inverse
            cc[zl, :, at] = heat
    rim_start(1, ix)
    share_copy = pltpu.make_async_copy(R, shares_out, osem)
    share_copy.start()
    rim_wait(0, bx)

    early = jnp.sum(sum_wait(0, 1), axis=1, keepdims=True)
    norm = early[0:1]
    weight = early[2:3]
    mean_c = early[2:3] * param[M]
    mean_i = early[2:3] * param[0]
    for i in range(1, M):
        weight = weight + early[2 + i : 3 + i]
        mean_c = mean_c + early[2 + i : 3 + i] * param[M + i]
        mean_i = mean_i + early[2 + i : 3 + i] * param[i]
    sigma = mean_c / weight + early[1:2] / norm * weight / mean_i
    per = 1.0 / sigma

    def beside(i, f, zl, g):
        w = f[zl, 8 + 8 * g : 16 + 8 * g, :]
        above = f[zl, 7 + 8 * g : 15 + 8 * g, :]
        below = f[zl, 9 + 8 * g : 17 + 8 * g, :]
        lane = lanes((8, 128))
        hl = pltpu.roll(hr_col[i, 0, 8 * g : 8 * g + 8, :], 1 + zl, 1)
        hr = pltpu.roll(hr_col[i, 1, 8 * g : 8 * g + 8, :], 127 - zl, 1)
        left = pltpu.roll(w, 1, 1)
        right = pltpu.roll(w, 767, 1)
        left = jnp.concatenate([jnp.where(lane == 0, hl, left[:, 0:128]), left[:, 128:]], axis=1)
        right = jnp.concatenate(
            [right[:, 0:640], jnp.where(lane == 127, hr, right[:, 640:])], axis=1
        )
        return w, above, below, left, right

    def apply(i, f, out, out_row):
        odd = jnp.zeros((8, 768), F32)
        even = jnp.zeros((8, 768), F32)
        for zl in range(2):
            for g in range(6):
                at = slice(8 * g, 8 * g + 8)
                w, above, below, left, right = beside(i, f, zl, g)
                other = f[1 - zl, 8 + 8 * g : 16 + 8 * g, :]
                v = cc[zl, at, :] * w
                v = v + fz[at, :] * (w - other)
                v = v + fu[zl, at, :] * (w - above) + fd[zl, at, :] * (w - below)
                v = v + fl[zl, at, :] * (w - left) + fr[zl, at, :] * (w - right)
                out[zl, out_row + 8 * g : out_row + 8 * g + 8, :] = v
                odd = odd + w * v
                even = even + v * v
        return rows_of(fold(odd)), rows_of(fold(even))

    rim_wait(1, ix)
    zero, one = jnp.float32(0.0), jnp.float32(1.0)
    top = jnp.where(r == 0, zero, one)
    bottom = jnp.where(r == 63, zero, one)
    first = jnp.where(c == 0, zero, one)
    last = jnp.where(c == 3, zero, one)
    twice = jnp.broadcast_to(2.0 * per, (8, 768))
    for zl in range(2):
        for g in range(6):
            at = slice(8 * g, 8 * g + 8)
            w, above, below, left, right = beside(1, ix, zl, g)
            f = twice / (w + above)
            fu[zl, at, :] = f * jnp.where(row8 == 0, top, one) if g == 0 else f
            f = twice / (w + below)
            fd[zl, at, :] = f * jnp.where(row8 == 7, bottom, one) if g == 5 else f
            fl[zl, at, :] = twice / (w + left) * jnp.where(lane8 == 0, first, one)
            fr[zl, at, :] = twice / (w + right) * jnp.where(lane8 == 767, last, one)
            if zl == 0:
                fz[at, :] = twice / (w + ix[1, 8 + 8 * g : 16 + 8 * g, :])
            cc[zl, at, :] = cc[zl, at, :] * per - 1.0

    tile_a[1] = jnp.zeros((8, 128), F32)
    s1, s2 = apply(0, bx, v1, 8)
    rim_start(2, v1)
    tile_a[1, 0:1, :] = s1
    tile_a[1, 1:2, :] = s2
    rim_wait(2, v1)
    s1, s2 = apply(2, v1, v2, 8)
    rim_start(3, v2)
    tile_a[1, 2:3, :] = s1
    tile_a[1, 3:4, :] = s2
    rim_wait(3, v2)
    s1, s2 = apply(3, v2, v3, 0)
    tile_a[1, 4:5, :] = s1
    sum_start(1, 0)
    tile_b[1] = sum_wait(1, 0)
    sum_start(1, 1)
    sums = jnp.sum(sum_wait(1, 1), axis=1, keepdims=True)
    mom = [norm] + [sums[i : i + 1] for i in range(5)]

    def inner(p, q):
        total = None
        for i, pi in enumerate(p):
            for j, qj in enumerate(q):
                term = pi * qj * mom[i + j]
                total = term if total is None else total + term
        return total

    def combine(p, q, s):
        size = max(len(p), len(q))
        out = []
        for i in range(size):
            if i < len(p) and i < len(q):
                out.append(p[i] + s * q[i])
            else:
                out.append(p[i] if i < len(p) else s * q[i])
        return out

    unit = jnp.ones((1, 1), F32)
    x, res, direction, rr = [], [unit], [unit], norm
    for it in range(3):
        n = len(direction)
        applied = [direction[0] * sigma]
        applied += [(direction[i] + direction[i - 1]) * sigma for i in range(1, n)]
        applied += [direction[n - 1] * sigma]
        alpha = rr / inner(direction, applied)
        x = combine(x, direction, alpha)
        res = combine(res, applied, -alpha)
        if it < 2:
            new = inner(res, res)
            direction = combine(res, direction, new / rr)
            rr = new

    for zl in range(2):
        for g in range(6):
            at = slice(8 * g, 8 * g + 8)
            ext = slice(8 + 8 * g, 16 + 8 * g)
            base = (bx[zl, ext, :], v1[zl, ext, :], v2[zl, ext, :], v3[zl, at, :])
            out = x[0] * base[0]
            for i in range(1, 3):
                out = out + x[i] * base[i]
            x_out[zl, at, :] = out
            out = res[0] * base[0]
            for i in range(1, 4):
                out = out + res[i] * base[i]
            r_out[zl, at, :] = out

    share_copy.wait()
    sent = sbuf.at[0:63]
    pltpu.make_async_copy(sent, sent, ssem).wait()
    sent = rb1.at[0:48]
    pltpu.make_async_copy(sent, sent, ssem2).wait()
    for i in range(2):
        for stage in range(2):
            sent = got_a.at[i, 0:15]
            pltpu.make_async_copy(sent, sent, ts_sem.at[i, stage]).wait()


def per_device(
    fractions_source,
    x_source_edges,
    x_target_edges,
    y_source_edges,
    y_target_edges,
    conductivity_table,
    capacity,
    thermal_source_term,
):
    def sides(edges, width):
        edges = edges.astype(F32)
        return [edges[:-1].reshape(NQ, width), edges[1:].reshape(NQ, width)]

    src_rows = jnp.concatenate(sides(y_source_edges, 128) + sides(x_source_edges, 128), axis=0)
    tgt_cols = jnp.concatenate(sides(y_target_edges, 96) + sides(x_target_edges, 96), axis=0).T
    param = jnp.concatenate([16.0 / conductivity_table.astype(F32), capacity])
    field = jax.ShapeDtypeStruct((2, TB, 768), F32)
    vmem = pl.BlockSpec(memory_space=pltpu.VMEM)
    anywhere = pl.BlockSpec(memory_space=pl.ANY)
    ext = VM((2, 64, 768), F32)
    inner = VM((2, TB, 768), F32)
    return pl.pallas_call(
        kernel,
        out_shape=(jax.ShapeDtypeStruct((2 * M, TB, 768), F32), field, field),
        in_specs=[anywhere, vmem, vmem, pl.BlockSpec(memory_space=pltpu.SMEM), vmem],
        out_specs=(anywhere, vmem, vmem),
        scratch_shapes=[
            VM((NQ, 3, 64, 128), F32),
            VM((96, 128), F32),
            VM((96, 128), BF16), VM((96, 128), BF16),
            VM((32, 128), BF16), VM((32, 128), BF16),
            VM((64, TB, 128), F32), VM((64, TB, 128), F32), VM((64, TB, 128), F32),
            VM((2 * M, TB, 768), F32),
            ext, ext, ext, ext, inner, inner,
            inner, inner, inner, inner, VM((TB, 768), F32),
            VM((4, 2, 2, 768), F32), VM((4, 2, 2, 768), F32),
            VM((4, 2, TB, 128), F32), VM((4, 2, TB, 128), F32),
            VM((3, 8, 128), F32),
            VM((2, 8, 128), F32), VM((2, 16, 8, 128), F32),
            VM((2, 8, 128), F32), VM((2, 16, 8, 128), F32),
            DMA((NQ,)), DMA, DMA((64,)), DMA, DMA((64,)),
            DMA((4, 4)), DMA((4, 4)), DMA((2, 2)), DMA((2, 2)), DMA,
        ],
        compiler_params=pltpu.CompilerParams(
            collective_id=0, has_side_effects=True, vmem_limit_bytes=48 * 2**20
        ),
    )(fractions_source, src_rows, tgt_cols, param, thermal_source_term)


def solution(mesh):
    placed = (P("col", "row", None), P(), P(), P(), P(), P(), P(), P(None, "row", "col"))
    return jax.shard_map(
        per_device,
        mesh=mesh,
        in_specs=placed,
        out_specs=(P(None, "row", "col"), P(None, "row", "col"), P(None, "row", "col")),
        check_vma=False,
    )
```

time: 655 us -> 102 us (0.16); the launches traced: 647 us -> 102 us
  blocking collectives: 373 us -> 0 us
  Pallas kernels: 0 us -> 90.4 us
  waiting for transfers between devices: 85.3 us -> 0 us
  local copies, waits for them, and re-layouts: 64.6 us -> 6.35 us
  starting transfers between devices: 55.2 us -> 0 us
  matrix products: 30.9 us -> 0 us
  other arithmetic: 29.4 us -> 4.42 us
  between operations: 8.01 us -> 0.68 us
    psum x5 -> x0, blocking collectives: 373 us -> none  [the longest x3 222 us: squares(): lax.psum(jnp.sum(remaining_defect * remaining_defect), ('row', 'col'))]
    pallas_call x0 -> x1, Pallas kernels: none -> 90.4 us  [per_device(): pl.pallas_call(kernel, out_shape=(jax.ShapeDtypeStruct((2 * M, TB, 768),...]
    all_to_all x2 -> x0, waiting for transfers between devices: 73.5 us -> none  [the longest x1 56 us: per_device(): lax.all_to_all(along_y, 'row', split_axis=2, concat_axis=1, tiled=True)]
    ppermute x16 -> x0, starting transfers between devices: 37.4 us -> none  [the longest x8 24.6 us: extended(): lax.ppermute(tail, axis, [(i, (i + 1) % count) for i in range(ends)])]
    dot_general x2 -> x0, matrix products: 30.9 us -> none  [the longest x1 16.5 us: per_device(): jnp.einsum('psbu,bvu->psbv', source_grid, vertical_factor, precision=lax....]
    unnamed x26 -> x7, local copies, waits for them, and re-layouts: 32.4 us -> 5.48 us
    all_to_all x2 -> x0, starting transfers between devices: 17.8 us -> none  [the longest x1 13.6 us: per_device(): lax.all_to_all(along_y, 'row', split_axis=2, concat_axis=1, tiled=True)]
    reshape x3 -> x9, local copies, waits for them, and re-layouts: 16.6 us -> 0.71 us  [sides(): return [edges[:-1].reshape(NQ, width), edges[1:].reshape(NQ, width)]]
  transfers between devices with their start and end apart: 18 -> 0, of which waited for: 6 -> 0; matrix products, arithmetic and copies ran while one was open for 5% -> 0% of each run, Pallas kernels for 0% -> 0%
where the time goes in v1:
time: 102 us
  Pallas kernels  90.4 us (89%)
  local copies, waits for them, and re-layouts  6.35 us (6%)
  other arithmetic  4.42 us (4%)
    pallas_call x1, Pallas kernels, per_device(): pl.pallas_call(kernel, out_shape=(jax.ShapeDtypeStruct((2 * M, TB, 768),...  90.4 us
    unnamed x7, local copies, waits for them, and re-layouts  5.48 us
    convert_element_type x4, other arithmetic, sides(): edges = edges.astype(F32)  2.91 us

profile of v1, /device:TPU:1, one launch (start us, length us, event | category | flops | bytes accessed | tf_op | source)
XLA Modules:
  0.0 101.8 jit_solution(16823750401789384712)
XLA Ops:
  0.6 0.7 convert_divide_fusion
  1.3 0.7 pad_maximum_fusion.1.param
  2.0 0.7 convert_element_type.18
  2.7 0.1 fusion.1
  2.8 0.1 reshape.36
  2.9 0.1 reshape.37
  3.0 0.7 convert_element_type.17
  3.7 0.1 fusion
  3.8 0.1 reshape.34
  3.8 0.1 reshape.35
  3.9 0.7 convert_element_type.16
  4.6 0.7 convert_element_type.15
  5.4 0.1 slice_bitcast_fusion.1
  5.5 0.1 copy.12
  5.5 0.1 copy.11
  5.6 0.1 copy.14
  5.7 0.1 copy.13
  5.8 0.1 maximum_bitcast_fusion.tgt_cols
  5.9 0.0 copy-start
  6.0 1.9 %copy-done = f32[3,64,4096]{2,1,0:T(8,128)S(1)} copy-done((f32[3,64,4096]{2,1,0:T(8,128)S(1)}, f32[3,64,4096]{2,1,0:T(8,128)}, u32[]{:S(2)}) %copy-start) | copy-done | bytes 3145752
  7.8 0.0 copy-start.1
  7.8 1.0 copy-done.1
  8.8 90.4 %shard_map.103 = (f32[12,48,768]{2,1,0:T(8,128)S(1)}, f32[2,48,768]{2,1,0:T(8,128)S(1)}, f32[2,48,768]{2,1,0:T(8,128)S(1)}) custom-call(f32[3,64,4096]{2,1,0:T(8,128)S(1)} %copy-done, f32[128,128]{1,0:T(8,128)S(1)} %pad_maximum_fusion.src_rows, f32[96,128]{1,0:T(8,128)S(1)} %maximum_bitcast_fusion.tgt_cols, f32[12]{0:T(128)S(1)} %pad_maximum_fusion.1.param, ...), custom_call_target="tpu_custom_call" | custom-call | tf_op jit(solution)/shard_map/pallas_call | solution.py:516
  99.2 1.2 %copy.18 = f32[12,48,768]{2,1,0:T(8,128)} copy(f32[12,48,768]{2,1,0:T(8,128)S(1)} %get-tuple-element.16) | data formatting | bytes 3538944
  100.4 0.7 copy.19
  101.1 0.7 copy.20
  (1 shorter events, 0.0 us)
Async XLA Ops:
  5.9 1.9 %copy-start = (f32[3,64,4096]{2,1,0:T(8,128)S(1)}, f32[3,64,4096]{2,1,0:T(8,128)}, u32[]{:S(2)}) copy-start(f32[3,64,4096]{2,1,0:T(8,128)} %frac.1) | copy-start | bytes 9437188
  7.8 1.0 copy-start.1

commit v2 on v1

--- a/solution.py
+++ b/solution.py
@@ -8,8 +8,9 @@
 M = 6
 TB = 48
 NQ = 32
-LAG_FORWARD = 6
-LAG_MERGE = 12
+AHEAD = 14
+LAG_FORWARD = 8
+LAG_MERGE = 14
 MESH = pl.DeviceIdType.MESH
 F32 = jnp.float32
 BF16 = jnp.bfloat16
@@ -40,10 +41,11 @@
 
 
 def kernel(
-    frac, src_rows, tgt_cols, param, b_ref, shares_out, x_out, r_out,
-    fbuf, wxp, wah, wal, wbh, wbl, sbuf, rb1, rb2, R, bx, ix, v1, v2, v3, cc,
+    frac, xs_edges, xt_edges, ys_edges, yt_edges, table_in, capacity_in, b_ref, R, x_out, r_out,
+    xs_line, xt_line, ys_line, yt_line, xs_rows, xt_rows, ys_rows, yt_rows,
+    table, capacity, fbuf, wxp, wah, wal, wbh, wbl, sbuf, rb1, rb2, bx, ix, v1, v2, v3, cc,
     fu, fd, fl, fr, fz, hs_row, hr_row, hs_col, hr_col, acc, tile_a, got_a, tile_b, got_b,
-    fsem, ssem, rsem1, ssem2, rsem2, hs_sem, hr_sem, ts_sem, tr_sem, osem,
+    esem, fsem, ssem, rsem1, ssem2, rsem2, hs_sem, hr_sem, ts_sem, tr_sem,
 ):
     r = lax.axis_index("row")
     c = lax.axis_index("col")
@@ -52,6 +54,14 @@
     y, z = chip // 8, chip % 8
     half = c % 2
 
+    lines = ((xs_edges, xs_line), (xt_edges, xt_line), (ys_edges, ys_line), (yt_edges, yt_line))
+    early_copies = [pltpu.make_async_copy(a, b, esem.at[i]) for i, (a, b) in enumerate(lines)]
+    early_copies.append(pltpu.make_async_copy(b_ref, bx.at[:, 8:56, :], esem.at[4]))
+    early_copies.append(pltpu.make_async_copy(table_in, table, esem.at[5]))
+    early_copies.append(pltpu.make_async_copy(capacity_in, capacity, esem.at[6]))
+    for copy in early_copies:
+        copy.start()
+
     def fetch(k):
         dy, dz = offsets(k)
         q = ((y + dy) % 4) * 8 + (z + dz) % 8
@@ -80,16 +90,31 @@
     def _(j):
         greet((r + 16 * (1 + j // 3)) % 64, (c + 1 + j % 3) % 4)
 
-    def pair_weights(low, high, cols):
-        t_low, t_high = cols[:, 0:1], cols[:, 32:33]
+    for i, (line, rows) in enumerate(
+        ((xs_line, xs_rows), (xt_line, xt_rows), (ys_line, ys_rows), (yt_line, yt_rows))
+    ):
+        early_copies[i].wait()
+        for q in range(line.shape[0] // 128):
+            part = line[128 * q : 128 * (q + 1)]
+            rows[q : q + 1, :] = part.astype(F32).reshape(1, 128)
+        q = line.shape[0] // 128
+        rows[q : q + 1, 0:1] = line[128 * q : 128 * q + 1].astype(F32).reshape(1, 1)
+
+    lane1 = lanes((1, 128))
+
+    def pair_weights(src, tgt, q):
+        low = src[pl.ds(q, 1), :]
+        high = pltpu.roll(jnp.where(lane1 == 0, src[pl.ds(q + 1, 1), :], low), 127, 1)
+        row = 96 * q // 128
+        off = 96 * q % 128
+        line = jnp.where(lane1 >= off, tgt[pl.ds(row, 1), :], tgt[pl.ds(row + 1, 1), :])
+        line = pltpu.roll(line, (128 - off) % 128, 1)
+        cols = jnp.broadcast_to(line, (128, 128)).T
+        t_low, t_high = cols[0:96], cols[1:97]
         shared = jnp.maximum(jnp.minimum(high, t_high) - jnp.maximum(low, t_low), 0.0)
         return shared / (t_high - t_low)
 
-    wxp[...] = pair_weights(
-        src_rows[pl.ds(64 + chip, 1), :],
-        src_rows[pl.ds(96 + chip, 1), :],
-        pltpu.roll(tgt_cols[...], 64 - chip, 1),
-    )
+    wxp[...] = pair_weights(xs_rows, xt_rows, chip)
     wx = wxp[pl.ds(pl.multiple_of(TB * core, 8), TB), :]
     wx = pltpu.roll(wx, 64 * core, 1)
     wx64 = pltpu.roll(wx, 64, 1)
@@ -102,8 +127,8 @@
     wbh[...] = hi
     wbl[...] = lo
 
-    for zl in range(2):
-        bx[zl, 8:56, :] = b_ref[zl]
+    for copy in early_copies[4:]:
+        copy.wait()
     acc[...] = jnp.zeros_like(acc)
 
     def fold(a):
@@ -135,8 +160,6 @@
     tile_a[0, 0:1, :] = rows_of(fold(square))
     tile_a[0, 1:2, :] = rows_of(fold(rough))
 
-    pl.semaphore_wait(barrier, 75)
-
     lane48 = lanes((TB, 128))
 
     def rim_copies(i):
@@ -172,8 +195,6 @@
             f[zl, 7:8, :] = hr_row[i, 0, zl : zl + 1, :]
             f[zl, 56:57, :] = hr_row[i, 1, zl : zl + 1, :]
 
-    rim_start(0, bx)
-
     spot_a = r % 16
     spot_b = y * 4 + c
 
@@ -210,10 +231,7 @@
     def compute(k):
         dy, dz = offsets(k)
         q = ((y + dy) % 4) * 8 + (z + dz) % 8
-        wy = pair_weights(
-            src_rows[pl.ds(q, 1), :], src_rows[pl.ds(32 + q, 1), :],
-            pltpu.roll(tgt_cols[...], (128 - q) % 128, 1),
-        )
+        wy = pair_weights(ys_rows, yt_rows, q)
         wyh, wyl = split(wy)
         fetch(k).wait()
         f = fbuf[k]
@@ -296,17 +314,29 @@
                         there = pl.ds(pl.multiple_of(t1 * 128, 128), 128)
                         R[m, :, there] = jnp.where(lane48 < off + width - 128, turned, R[m, :, there])
 
+    @pl.loop(0, AHEAD)
+    def _(k):
+        compute(k)
+
+    pl.semaphore_wait(barrier, 75)
+
+    @pl.loop(0, AHEAD)
+    def _(k):
+        send(k)
+
+    rim_start(0, bx)
+
     @pl.loop(0, NQ + LAG_MERGE)
     def _(it):
-        @pl.when(it < NQ)
+        @pl.when(it < NQ - AHEAD)
         def _():
-            compute(it)
-
-        @pl.when(jnp.logical_and(it >= 1, it <= NQ))
+            compute(it + AHEAD)
+
+        @pl.when(jnp.logical_and(it >= 1, it <= NQ - AHEAD))
         def _():
-            send(it - 1)
-
-        @pl.when(it == NQ)
+            send(it + AHEAD - 1)
+
+        @pl.when(it == NQ - AHEAD)
         def _():
             hf = half.astype(F32)
             for p in range(3):
@@ -315,7 +345,7 @@
                 tile_a[0, 5 + p : 6 + p, :] = v * hf
             sum_start(0, 0)
 
-        @pl.when(it == NQ + 5)
+        @pl.when(it == NQ - AHEAD + 6)
         def _():
             tile_b[0] = sum_wait(0, 0)
             sum_start(0, 1)
@@ -327,6 +357,9 @@
         @pl.when(it >= LAG_MERGE)
         def _():
             merge(it - LAG_MERGE)
+
+    param = [16.0 / jnp.full((1, 128), table[i].astype(F32)) for i in range(M)]
+    param += [jnp.full((1, 128), capacity[i]) for i in range(M)]
 
     for t in range(6):
         at = slice(128 * t, 128 * (t + 1))
@@ -345,10 +378,9 @@
             ix[zl, 8:56, at] = inverse
             cc[zl, :, at] = heat
     rim_start(1, ix)
-    share_copy = pltpu.make_async_copy(R, shares_out, osem)
-    share_copy.start()
     rim_wait(0, bx)
 
+    param = [a[:, 0:1] for a in param]
     early = jnp.sum(sum_wait(0, 1), axis=1, keepdims=True)
     norm = early[0:1]
     weight = early[2:3]
@@ -480,7 +512,6 @@
                 out = out + res[i] * base[i]
             r_out[zl, at, :] = out
 
-    share_copy.wait()
     sent = sbuf.at[0:63]
     pltpu.make_async_copy(sent, sent, ssem).wait()
     sent = rb1.at[0:48]
@@ -489,6 +520,15 @@
         for stage in range(2):
             sent = got_a.at[i, 0:15]
             pltpu.make_async_copy(sent, sent, ts_sem.at[i, stage]).wait()
+
+
+def put_out(*refs):
+    sem = refs[6]
+    copies = [pltpu.make_async_copy(refs[i], refs[3 + i], sem.at[i]) for i in range(3)]
+    for copy in copies:
+        copy.start()
+    for copy in copies:
+        copy.wait()
 
 
 def per_device(
@@ -501,30 +541,27 @@
     capacity,
     thermal_source_term,
 ):
-    def sides(edges, width):
-        edges = edges.astype(F32)
-        return [edges[:-1].reshape(NQ, width), edges[1:].reshape(NQ, width)]
-
-    src_rows = jnp.concatenate(sides(y_source_edges, 128) + sides(x_source_edges, 128), axis=0)
-    tgt_cols = jnp.concatenate(sides(y_target_edges, 96) + sides(x_target_edges, 96), axis=0).T
-    param = jnp.concatenate([16.0 / conductivity_table.astype(F32), capacity])
     field = jax.ShapeDtypeStruct((2, TB, 768), F32)
     vmem = pl.BlockSpec(memory_space=pltpu.VMEM)
-    anywhere = pl.BlockSpec(memory_space=pl.ANY)
+    hbm = pl.BlockSpec(memory_space=pltpu.HBM)
+    shapes = (jax.ShapeDtypeStruct((2 * M, TB, 768), F32), field, field)
     ext = VM((2, 64, 768), F32)
     inner = VM((2, TB, 768), F32)
-    return pl.pallas_call(
+    made = pl.pallas_call(
         kernel,
-        out_shape=(jax.ShapeDtypeStruct((2 * M, TB, 768), F32), field, field),
-        in_specs=[anywhere, vmem, vmem, pl.BlockSpec(memory_space=pltpu.SMEM), vmem],
-        out_specs=(anywhere, vmem, vmem),
+        out_shape=shapes,
+        in_specs=[hbm] * 8,
+        out_specs=(vmem, vmem, vmem),
         scratch_shapes=[
+            VM((4097,), jnp.int32), VM((3073,), jnp.int32),
+            VM((4097,), jnp.int32), VM((3073,), jnp.int32),
+            VM((40, 128), F32), VM((32, 128), F32), VM((40, 128), F32), VM((32, 128), F32),
+            pltpu.SMEM((M,), jnp.int32), pltpu.SMEM((M,), F32),
             VM((NQ, 3, 64, 128), F32),
             VM((96, 128), F32),
             VM((96, 128), BF16), VM((96, 128), BF16),
             VM((32, 128), BF16), VM((32, 128), BF16),
             VM((64, TB, 128), F32), VM((64, TB, 128), F32), VM((64, TB, 128), F32),
-            VM((2 * M, TB, 768), F32),
             ext, ext, ext, ext, inner, inner,
             inner, inner, inner, inner, VM((TB, 768), F32),
             VM((4, 2, 2, 768), F32), VM((4, 2, 2, 768), F32),
@@ -532,13 +569,29 @@
             VM((3, 8, 128), F32),
             VM((2, 8, 128), F32), VM((2, 16, 8, 128), F32),
             VM((2, 8, 128), F32), VM((2, 16, 8, 128), F32),
-            DMA((NQ,)), DMA, DMA((64,)), DMA, DMA((64,)),
-            DMA((4, 4)), DMA((4, 4)), DMA((2, 2)), DMA((2, 2)), DMA,
+            DMA((7,)), DMA((NQ,)), DMA, DMA((64,)), DMA, DMA((64,)),
+            DMA((4, 4)), DMA((4, 4)), DMA((2, 2)), DMA((2, 2)),
         ],
         compiler_params=pltpu.CompilerParams(
             collective_id=0, has_side_effects=True, vmem_limit_bytes=48 * 2**20
         ),
-    )(fractions_source, src_rows, tgt_cols, param, thermal_source_term)
+    )(
+        *[
+            pltpu.with_memory_space_constraint(a, pltpu.HBM)
+            for a in (
+                fractions_source, x_source_edges, x_target_edges, y_source_edges, y_target_edges,
+                conductivity_table, capacity, thermal_source_term,
+            )
+        ]
+    )
+    return pl.pallas_call(
+        put_out,
+        out_shape=shapes,
+        in_specs=[pl.BlockSpec(memory_space=pl.ANY)] * 3,
+        out_specs=(hbm, hbm, hbm),
+        scratch_shapes=[DMA((3,))],
+        compiler_params=pltpu.CompilerParams(vmem_limit_bytes=2**20),
+    )(*made)
 
 
 def solution(mesh):

time: 102 us -> 97.1 us (0.952)
  local copies, waits for them, and re-layouts: 6.35 us -> 0 us
  Pallas kernels: 90.4 us -> 96.4 us
  other arithmetic: 4.42 us -> 0 us
    pallas_call x1 -> x2, Pallas kernels: 90.4 us -> 96.4 us  [the longest x1 95 us: per_device(): pl.pallas_call(kernel, out_shape=shapes, in_specs=[hbm] * 8, out_specs=(v...]
    unnamed x7 -> x0, local copies, waits for them, and re-layouts: 5.48 us -> none
    convert_element_type x4 -> x0, other arithmetic: 2.91 us -> none  [sides(): edges = edges.astype(F32)]
where the time goes in v2:
time: 97.1 us
  Pallas kernels  96.4 us (99%)
    pallas_call x1, Pallas kernels, per_device(): pl.pallas_call(kernel, out_shape=shapes, in_specs=[hbm] * 8, out_specs=(v...  95 us

profile of v2, /device:TPU:1, one launch (start us, length us, event | category | flops | bytes accessed | tf_op | source)
XLA Modules:
  0.0 97.1 jit_solution(10286655546705954657)
XLA Ops:
  0.6 95.0 %shard_map.103 = (f32[12,48,768]{2,1,0:T(8,128)S(1)}, f32[2,48,768]{2,1,0:T(8,128)S(1)}, f32[2,48,768]{2,1,0:T(8,128)S(1)}) custom-call(f32[3,64,4096]{2,1,0:T(8,128)} %frac.1, s32[4097]{0:T(1024)} %xs_edges.1, s32[3073]{0:T(1024)} %xt_edges.1, s32[4097]{0:T(1024)} %ys_edges.1, s32[3073]{0:T(1024)} %yt_edges.1, s32[6]{0:T(128)} %table_in.1, f32[6]{0:T(128)} %capacity_in.1, ...), custom_call_target="tpu_custom_call" | custom-call | tf_op jit(solution)/shard_map/pallas_call | solution.py:550
  95.6 1.4 %shard_map.104 = (f32[12,48,768]{2,1,0:T(8,128)}, f32[2,48,768]{2,1,0:T(8,128)}, f32[2,48,768]{2,1,0:T(8,128)}) custom-call(f32[12,48,768]{2,1,0:T(8,128)S(1)} %get-tuple-element.6.refs_0_, f32[2,48,768]{2,1,0:T(8,128)S(1)} %get-tuple-element.7.refs_1_, f32[2,48,768]{2,1,0:T(8,128)S(1)} %get-tuple-element.8.refs_2_), custom_call_target="tpu_custom_call" | custom-call | tf_op jit(solution)/shard_map/pallas_call | solution.py:587

commit v3 on v2

--- a/solution.py
+++ b/solution.py
@@ -8,9 +8,9 @@
 M = 6
 TB = 48
 NQ = 32
-AHEAD = 14
-LAG_FORWARD = 8
-LAG_MERGE = 14
+GROUP = 4
+WINDOW = 20
+LAG_MERGE = 16
 MESH = pl.DeviceIdType.MESH
 F32 = jnp.float32
 BF16 = jnp.bfloat16
@@ -23,17 +23,14 @@
     return high, (a - high.astype(F32)).astype(BF16)
 
 
-def product(ah, al, bh, bl, dims):
-    def dot(p, q):
-        return lax.dot_general(p, q, (dims, ((), ())), preferred_element_type=F32)
-
-    return dot(ah, bh) + (dot(ah, bl) + dot(al, bh))
-
-
-def offsets(k):
+def dot(a, b, dims):
+    return lax.dot_general(a, b, (dims, ((), ())), preferred_element_type=F32)
+
+
+def offsets(k, c):
     g, s = k // 8, k % 2
     dz = jnp.where(s == 0, 4 - g, jnp.where(g == 0, 0, 4 + g))
-    return (k // 2) % 4, dz
+    return (k // 2 + c) % 4, dz
 
 
 def lanes(shape):
@@ -43,7 +40,7 @@
 def kernel(
     frac, xs_edges, xt_edges, ys_edges, yt_edges, table_in, capacity_in, b_ref, R, x_out, r_out,
     xs_line, xt_line, ys_line, yt_line, xs_rows, xt_rows, ys_rows, yt_rows,
-    table, capacity, fbuf, wxp, wah, wal, wbh, wbl, sbuf, rb1, rb2, bx, ix, v1, v2, v3, cc,
+    table, capacity, fbuf, wxp, wx_all, sbuf, rb1, rb2, bx, ix, v1, v2, v3, cc,
     fu, fd, fl, fr, fz, hs_row, hr_row, hs_col, hr_col, acc, tile_a, got_a, tile_b, got_b,
     esem, fsem, ssem, rsem1, ssem2, rsem2, hs_sem, hr_sem, ts_sem, tr_sem,
 ):
@@ -63,7 +60,7 @@
         copy.start()
 
     def fetch(k):
-        dy, dz = offsets(k)
+        dy, dz = offsets(k, c)
         q = ((y + dy) % 4) * 8 + (z + dz) % 8
         return pltpu.make_async_copy(
             frac.at[:, :, pl.ds(pl.multiple_of(q * 128, 128), 128)], fbuf.at[k], fsem.at[k]
@@ -80,11 +77,14 @@
 
     @pl.loop(1, 64)
     def _(j):
-        greet((r + j) % 64, c)
+        greet(16 * y + (r + j // 4) % 16, (c + j % 4) % 4)
 
     @pl.loop(1, 4)
     def _(j):
-        greet(r, (c + j) % 4)
+        greet((r + 16 * j) % 64, c)
+
+    greet((r + 1) % 64, c)
+    greet((r + 63) % 64, c)
 
     @pl.loop(0, 9)
     def _(j):
@@ -117,15 +117,18 @@
     wxp[...] = pair_weights(xs_rows, xt_rows, chip)
     wx = wxp[pl.ds(pl.multiple_of(TB * core, 8), TB), :]
     wx = pltpu.roll(wx, 64 * core, 1)
-    wx64 = pltpu.roll(wx, 64, 1)
-    wxp[0:TB, :] = wx64
-    hi, lo = split(jnp.concatenate([wx, wx64], axis=0))
-    wah[...] = hi
-    wal[...] = lo
+    wxp[0:TB, :] = wx
     third = wxp[pl.ds(pl.multiple_of(24 * half, 8), 24), :]
-    hi, lo = split(jnp.concatenate([third, jnp.zeros((8, 128), F32)], axis=0))
-    wbh[...] = hi
-    wbl[...] = lo
+    none = jnp.zeros((TB, 128), F32)
+    wx = jnp.concatenate(
+        [
+            jnp.concatenate([wx, pltpu.roll(wx, 64, 1), none[0:32]], axis=0),
+            jnp.concatenate([none, none, third, none[0:8]], axis=0),
+        ],
+        axis=1,
+    )[:, 0:192]
+    hi, lo = split(wx)
+    wx_all[...] = jnp.concatenate([hi, hi, lo], axis=1)
 
     for copy in early_copies[4:]:
         copy.wait()
@@ -228,131 +231,129 @@
             total = total + got[i, j]
         return total
 
-    def compute(k):
-        dy, dz = offsets(k)
-        q = ((y + dy) % 4) * 8 + (z + dz) % 8
-        wy = pair_weights(ys_rows, yt_rows, q)
-        wyh, wyl = split(wy)
-        fetch(k).wait()
-        f = fbuf[k]
-        for p in range(3):
-            acc[p] = acc[p] + jnp.sum(f[p].reshape(8, 8, 128), axis=0)
-        f = f.reshape(192, 128)
-        fh, fo = split(f)
-        nn = ((1,), (0,))
-        g0 = product(wah[...], wal[...], fh[0:128], fo[0:128], nn)
-        g1 = product(wbh[...], wbl[...], fh[64:192], fo[64:192], nn)
-        gh, go = split(jnp.concatenate([g0, g1], axis=0))
-        out = product(wyh, wyl, gh, go, ((1,), (1,)))
-        sbuf[2 * k] = out[0:TB]
-        sbuf[2 * k + 1] = out[TB : 2 * TB]
+    def weights_y(k):
+        dy, dz = offsets(k, c)
+        wh, wl = split(pair_weights(ys_rows, yt_rows, ((y + dy) % 4) * 8 + (z + dz) % 8))
+        return jnp.concatenate([wh, wh, wl], axis=1)
+
+    def compute(i):
+        steps = [GROUP * i + j for j in range(GROUP)]
+        for k in steps:
+            fetch(k).wait()
+        wy = [weights_y(k) for k in steps]
+        cells = [fbuf[k] for k in steps]
+        for f in cells:
+            for p in range(3):
+                acc[p] = acc[p] + jnp.sum(f[p].reshape(8, 8, 128), axis=0)
+        outs = []
+        for f, w in zip(cells, wy):
+            fh, fl = split(f.reshape(192, 128))
+            g = dot(wx_all[...], jnp.concatenate([fh, fl, fh], axis=0), ((1,), (0,)))
+            gh, gl = split(g)
+            outs.append(dot(w, jnp.concatenate([gh, gl, gh], axis=1), ((1,), (1,))))
+        for k, out in zip(steps, outs):
+            sbuf[2 * k] = out[0:TB]
+            sbuf[2 * k + 1] = out[TB : 2 * TB]
+
+    slot = c * 16 + z * 2 + core
+
+    def deliver(src, row, col):
+        mine = jnp.logical_and(row == r, col == c)
+
+        @pl.when(mine)
+        def _():
+            pltpu.make_async_copy(src, rb2.at[slot], rsem2.at[slot]).start()
+
+        @pl.when(jnp.logical_not(mine))
+        def _():
+            pltpu.make_async_remote_copy(
+                src_ref=src, dst_ref=rb2.at[slot], send_sem=ssem2, recv_sem=rsem2.at[slot],
+                device_id=(row, col), device_id_type=MESH,
+            ).start()
 
     def send(k):
-        dy, dz = offsets(k)
-        q = ((y + dy) % 4) * 8 + (z + dz) % 8
+        dy, dz = offsets(k, c)
         for s in range(2):
-            mine = jnp.logical_and(q == chip, core == s)
-
-            @pl.when(mine)
+            chunk = sbuf.at[2 * k + s]
+
+            @pl.when(dy == 0)
             def _():
-                pltpu.make_async_copy(
-                    sbuf.at[2 * k + s], rb1.at[2 * k + core], rsem1.at[2 * k + core]
-                ).start()
-
-            @pl.when(jnp.logical_not(mine))
+                deliver(chunk, 16 * y + (z + dz) % 8 * 2 + s, y)
+
+            @pl.when(dy != 0)
             def _():
                 pltpu.make_async_remote_copy(
-                    src_ref=sbuf.at[2 * k + s], dst_ref=rb1.at[2 * k + core],
-                    send_sem=ssem, recv_sem=rsem1.at[2 * k + core],
-                    device_id=(2 * q + s, c), device_id_type=MESH,
+                    src_ref=chunk, dst_ref=rb1.at[2 * k + s],
+                    send_sem=ssem, recv_sem=rsem1.at[2 * k + s],
+                    device_id=((r + 16 * dy) % 64, c), device_id_type=MESH,
                 ).start()
 
     def forward(k):
-        dy, dz = offsets(k)
-        to = (y - dy + 4) % 4
-        zs = (z - dz + 8) % 8
+        dy, dz = offsets(k, c)
+
+        @pl.when(dy != 0)
+        def _():
+            for s in range(2):
+                chunk = rb1.at[2 * k + s]
+                pltpu.make_async_copy(chunk, chunk, rsem1.at[2 * k + s]).wait()
+                deliver(chunk, 16 * y + (z + dz) % 8 * 2 + s, (y - dy + 4) % 4)
+
+    def merge(k):
+        cs = (y - k // 2 - c + 32) % 4
+        zs = (z - offsets(k, c)[1] + 8) % 8
         for s in range(2):
-            got = rb1.at[2 * k + s]
-            pltpu.make_async_copy(got, got, rsem1.at[2 * k + s]).wait()
-            slot = c * 16 + zs * 2 + s
-
-            @pl.when(to == c)
-            def _():
-                pltpu.make_async_copy(got, rb2.at[slot], rsem2.at[slot]).start()
-
-            @pl.when(to != c)
-            def _():
-                pltpu.make_async_remote_copy(
-                    src_ref=got, dst_ref=rb2.at[slot], send_sem=ssem2, recv_sem=rsem2.at[slot],
-                    device_id=(r, to), device_id_type=MESH,
-                ).start()
-
-    def merge(k):
-        dy, dz = offsets(k)
-        zs = (z - dz + 8) % 8
-
-        @pl.when((y - dy + 4) % 4 == c)
-        def _():
-            for cs in range(4):
-                for s in range(2):
-                    block = zs * 2 + s
-                    slot = cs * 16 + block
-                    got = rb2.at[slot]
-                    pltpu.make_async_copy(got, got, rsem2.at[slot]).wait()
-                    chunk = rb2[slot]
-                    for p in range(3):
-                        width = TB if p < 2 else 24
-                        pos = TB * block + (24 * (cs % 2) if p == 2 else 0)
-                        t0 = pos // 128
-                        off = pos % 128
-                        t1 = jnp.minimum(t0 + 1, 5)
-                        turned = pltpu.roll(chunk, (off + 256 - TB * p) % 128, 1)
-                        m = (cs // 2) * M + 3 * (cs % 2) + p
-                        here = pl.ds(pl.multiple_of(t0 * 128, 128), 128)
-                        inside = jnp.logical_and(lane48 >= off, lane48 < off + width)
-                        R[m, :, here] = jnp.where(inside, turned, R[m, :, here])
-                        there = pl.ds(pl.multiple_of(t1 * 128, 128), 128)
-                        R[m, :, there] = jnp.where(lane48 < off + width - 128, turned, R[m, :, there])
-
-    @pl.loop(0, AHEAD)
-    def _(k):
-        compute(k)
-
-    pl.semaphore_wait(barrier, 75)
-
-    @pl.loop(0, AHEAD)
+            block = zs * 2 + s
+            place = cs * 16 + block
+            got = rb2.at[place]
+            pltpu.make_async_copy(got, got, rsem2.at[place]).wait()
+            chunk = rb2[place]
+            for p in range(3):
+                width = TB if p < 2 else 24
+                pos = TB * block + (24 * (cs % 2) if p == 2 else 0)
+                t0 = pos // 128
+                off = pos % 128
+                t1 = jnp.minimum(t0 + 1, 5)
+                turned = pltpu.roll(chunk, (off + 256 - TB * p) % 128, 1)
+                m = (cs // 2) * M + 3 * (cs % 2) + p
+                here = pl.ds(pl.multiple_of(t0 * 128, 128), 128)
+                inside = jnp.logical_and(lane48 >= off, lane48 < off + width)
+                R[m, :, here] = jnp.where(inside, turned, R[m, :, here])
+                there = pl.ds(pl.multiple_of(t1 * 128, 128), 128)
+                R[m, :, there] = jnp.where(lane48 < off + width - 128, turned, R[m, :, there])
+
+    @pl.loop(0, NQ // GROUP)
+    def _(i):
+        compute(i)
+
+    hf = half.astype(F32)
+    for p in range(3):
+        v = rows_of(acc[p])
+        tile_a[0, 2 + p : 3 + p, :] = v * (1.0 - hf)
+        tile_a[0, 5 + p : 6 + p, :] = v * hf
+
+    pl.semaphore_wait(barrier, 77)
+
+    @pl.loop(0, WINDOW)
     def _(k):
         send(k)
 
     rim_start(0, bx)
+    sum_start(0, 0)
 
     @pl.loop(0, NQ + LAG_MERGE)
     def _(it):
-        @pl.when(it < NQ - AHEAD)
+        @pl.when(it < NQ)
         def _():
-            compute(it + AHEAD)
-
-        @pl.when(jnp.logical_and(it >= 1, it <= NQ - AHEAD))
+            forward(it)
+
+        @pl.when(it < NQ - WINDOW)
         def _():
-            send(it + AHEAD - 1)
-
-        @pl.when(it == NQ - AHEAD)
-        def _():
-            hf = half.astype(F32)
-            for p in range(3):
-                v = rows_of(acc[p])
-                tile_a[0, 2 + p : 3 + p, :] = v * (1.0 - hf)
-                tile_a[0, 5 + p : 6 + p, :] = v * hf
-            sum_start(0, 0)
-
-        @pl.when(it == NQ - AHEAD + 6)
+            send(it + WINDOW)
+
+        @pl.when(it == 10)
         def _():
             tile_b[0] = sum_wait(0, 0)
             sum_start(0, 1)
-
-        @pl.when(jnp.logical_and(it >= LAG_FORWARD, it < NQ + LAG_FORWARD))
-        def _():
-            forward(it - LAG_FORWARD)
 
         @pl.when(it >= LAG_MERGE)
         def _():
@@ -512,9 +513,9 @@
                 out = out + res[i] * base[i]
             r_out[zl, at, :] = out
 
-    sent = sbuf.at[0:63]
+    sent = sbuf.at[0:48]
     pltpu.make_async_copy(sent, sent, ssem).wait()
-    sent = rb1.at[0:48]
+    sent = rb2.at[0:63]
     pltpu.make_async_copy(sent, sent, ssem2).wait()
     for i in range(2):
         for stage in range(2):
@@ -559,8 +560,7 @@
             pltpu.SMEM((M,), jnp.int32), pltpu.SMEM((M,), F32),
             VM((NQ, 3, 64, 128), F32),
             VM((96, 128), F32),
-            VM((96, 128), BF16), VM((96, 128), BF16),
-            VM((32, 128), BF16), VM((32, 128), BF16),
+            VM((128, 576), BF16),
             VM((64, TB, 128), F32), VM((64, TB, 128), F32), VM((64, TB, 128), F32),
             ext, ext, ext, ext, inner, inner,
             inner, inner, inner, inner, VM((TB, 768), F32),

time: 97.1 us -> 84.7 us (0.87)
  Pallas kernels: 96.4 us -> 84 us
    pallas_call x1, Pallas kernels: 95 us -> 82.6 us  [per_device(): pl.pallas_call(kernel, out_shape=shapes, in_specs=[hbm] * 8, out_specs=(v...]
where the time goes in v3:
time: 84.7 us
  Pallas kernels  84 us (99%)
    pallas_call x1, Pallas kernels, per_device(): pl.pallas_call(kernel, out_shape=shapes, in_specs=[hbm] * 8, out_specs=(v...  82.6 us

profile of v3, /device:TPU:1, one launch (start us, length us, event | category | flops | bytes accessed | tf_op | source)
XLA Modules:
  0.0 84.7 jit_solution(5080827089839426769)
XLA Ops:
  0.6 82.6 %shard_map.103 = (f32[12,48,768]{2,1,0:T(8,128)S(1)}, f32[2,48,768]{2,1,0:T(8,128)S(1)}, f32[2,48,768]{2,1,0:T(8,128)S(1)}) custom-call(f32[3,64,4096]{2,1,0:T(8,128)} %frac.1, s32[4097]{0:T(1024)} %xs_edges.1, s32[3073]{0:T(1024)} %xt_edges.1, s32[4097]{0:T(1024)} %ys_edges.1, s32[3073]{0:T(1024)} %yt_edges.1, s32[6]{0:T(128)} %table_in.1, f32[6]{0:T(128)} %capacity_in.1, ...), custom_call_target="tpu_custom_call" | custom-call | tf_op jit(solution)/shard_map/pallas_call | solution.py:551
  83.2 1.4 %shard_map.104 = (f32[12,48,768]{2,1,0:T(8,128)}, f32[2,48,768]{2,1,0:T(8,128)}, f32[2,48,768]{2,1,0:T(8,128)}) custom-call(f32[12,48,768]{2,1,0:T(8,128)S(1)} %get-tuple-element.6.refs_0_, f32[2,48,768]{2,1,0:T(8,128)S(1)} %get-tuple-element.7.refs_1_, f32[2,48,768]{2,1,0:T(8,128)S(1)} %get-tuple-element.8.refs_2_), custom_call_target="tpu_custom_call" | custom-call | tf_op jit(solution)/shard_map/pallas_call | solution.py:587

commit v4 on v3

--- a/solution.py
+++ b/solution.py
@@ -9,7 +9,8 @@
 TB = 48
 NQ = 32
 GROUP = 4
-WINDOW = 20
+AHEAD = 12
+WINDOW = 12
 LAG_MERGE = 16
 MESH = pl.DeviceIdType.MESH
 F32 = jnp.float32
@@ -321,15 +322,9 @@
                 there = pl.ds(pl.multiple_of(t1 * 128, 128), 128)
                 R[m, :, there] = jnp.where(lane48 < off + width - 128, turned, R[m, :, there])
 
-    @pl.loop(0, NQ // GROUP)
+    @pl.loop(0, AHEAD // GROUP)
     def _(i):
         compute(i)
-
-    hf = half.astype(F32)
-    for p in range(3):
-        v = rows_of(acc[p])
-        tile_a[0, 2 + p : 3 + p, :] = v * (1.0 - hf)
-        tile_a[0, 5 + p : 6 + p, :] = v * hf
 
     pl.semaphore_wait(barrier, 77)
 
@@ -338,10 +333,22 @@
         send(k)
 
     rim_start(0, bx)
-    sum_start(0, 0)
 
     @pl.loop(0, NQ + LAG_MERGE)
     def _(it):
+        @pl.when(jnp.logical_and(it < NQ - AHEAD, it % GROUP == 0))
+        def _():
+            compute((it + AHEAD) // GROUP)
+
+        @pl.when(it == NQ - AHEAD)
+        def _():
+            hf = half.astype(F32)
+            for p in range(3):
+                v = rows_of(acc[p])
+                tile_a[0, 2 + p : 3 + p, :] = v * (1.0 - hf)
+                tile_a[0, 5 + p : 6 + p, :] = v * hf
+            sum_start(0, 0)
+
         @pl.when(it < NQ)
         def _():
             forward(it)
@@ -350,7 +357,7 @@
         def _():
             send(it + WINDOW)
 
-        @pl.when(it == 10)
+        @pl.when(it == NQ - AHEAD + 8)
         def _():
             tile_b[0] = sum_wait(0, 0)
             sum_start(0, 1)

time: 84.7 us -> 80.8 us (0.954)
  Pallas kernels: 84 us -> 80 us
    pallas_call x1, Pallas kernels: 82.6 us -> 78.6 us  [per_device(): pl.pallas_call(kernel, out_shape=shapes, in_specs=[hbm] * 8, out_specs=(v...]
where the time goes in v4:
time: 80.8 us; the launch traced here: 80.7 us
  Pallas kernels  80 us (99%)
    pallas_call x1, Pallas kernels, per_device(): pl.pallas_call(kernel, out_shape=shapes, in_specs=[hbm] * 8, out_specs=(v...  78.6 us

profile of v4, /device:TPU:1, one launch (start us, length us, event | category | flops | bytes accessed | tf_op | source)
XLA Modules:
  0.0 80.7 jit_solution(13308808937557921648)
XLA Ops:
  0.6 78.6 %shard_map.103 = (f32[12,48,768]{2,1,0:T(8,128)S(1)}, f32[2,48,768]{2,1,0:T(8,128)S(1)}, f32[2,48,768]{2,1,0:T(8,128)S(1)}) custom-call(f32[3,64,4096]{2,1,0:T(8,128)} %frac.1, s32[4097]{0:T(1024)} %xs_edges.1, s32[3073]{0:T(1024)} %xt_edges.1, s32[4097]{0:T(1024)} %ys_edges.1, s32[3073]{0:T(1024)} %yt_edges.1, s32[6]{0:T(128)} %table_in.1, f32[6]{0:T(128)} %capacity_in.1, ...), custom_call_target="tpu_custom_call" | custom-call | tf_op jit(solution)/shard_map/pallas_call | solution.py:558
  79.3 1.4 %shard_map.104 = (f32[12,48,768]{2,1,0:T(8,128)}, f32[2,48,768]{2,1,0:T(8,128)}, f32[2,48,768]{2,1,0:T(8,128)}) custom-call(f32[12,48,768]{2,1,0:T(8,128)S(1)} %get-tuple-element.6.refs_0_, f32[2,48,768]{2,1,0:T(8,128)S(1)} %get-tuple-element.7.refs_1_, f32[2,48,768]{2,1,0:T(8,128)S(1)} %get-tuple-element.8.refs_2_), custom_call_target="tpu_custom_call" | custom-call | tf_op jit(solution)/shard_map/pallas_call | solution.py:594

commit v5 on v4

--- a/solution.py
+++ b/solution.py
@@ -17,6 +17,7 @@
 BF16 = jnp.bfloat16
 VM = pltpu.VMEM
 DMA = pltpu.SemaphoreType.DMA
+IN = slice(128, 896)
 
 
 def split(a):
@@ -42,7 +43,7 @@
     frac, xs_edges, xt_edges, ys_edges, yt_edges, table_in, capacity_in, b_ref, R, x_out, r_out,
     xs_line, xt_line, ys_line, yt_line, xs_rows, xt_rows, ys_rows, yt_rows,
     table, capacity, fbuf, wxp, wx_all, sbuf, rb1, rb2, bx, ix, v1, v2, v3, cc,
-    fu, fd, fl, fr, fz, hs_row, hr_row, hs_col, hr_col, acc, tile_a, got_a, tile_b, got_b,
+    fu, fl, fz, hs_row, hr_row, hs_col, hr_col, acc, tile_a, got_a, tile_b, got_b,
     esem, fsem, ssem, rsem1, ssem2, rsem2, hs_sem, hr_sem, ts_sem, tr_sem,
 ):
     r = lax.axis_index("row")
@@ -54,7 +55,7 @@
 
     lines = ((xs_edges, xs_line), (xt_edges, xt_line), (ys_edges, ys_line), (yt_edges, yt_line))
     early_copies = [pltpu.make_async_copy(a, b, esem.at[i]) for i, (a, b) in enumerate(lines)]
-    early_copies.append(pltpu.make_async_copy(b_ref, bx.at[:, 8:56, :], esem.at[4]))
+    early_copies.append(pltpu.make_async_copy(b_ref, bx.at[:, 8:56, IN], esem.at[4]))
     early_copies.append(pltpu.make_async_copy(table_in, table, esem.at[5]))
     early_copies.append(pltpu.make_async_copy(capacity_in, capacity, esem.at[6]))
     for copy in early_copies:
@@ -84,8 +85,10 @@
     def _(j):
         greet((r + 16 * j) % 64, c)
 
-    greet((r + 1) % 64, c)
-    greet((r + 63) % 64, c)
+    for side in (1, 63):
+        greet((r + side) % 64, c)
+        greet((r + side) % 64, (c + 1) % 4)
+        greet((r + side) % 64, (c + 3) % 4)
 
     @pl.loop(0, 9)
     def _(j):
@@ -149,7 +152,7 @@
     square = jnp.zeros((8, 768), F32)
     rough = jnp.zeros((8, 768), F32)
     for g in range(6):
-        a = [bx[zl, 8 + 8 * g : 16 + 8 * g, :] for zl in range(2)]
+        a = [bx[zl, 8 + 8 * g : 16 + 8 * g, IN] for zl in range(2)]
         d = a[0] - a[1]
         rough = rough + d * d
         for zl in range(2):
@@ -157,7 +160,7 @@
             d = jnp.where(lane8 == 0, 0.0, a[zl] - pltpu.roll(a[zl], 1, 1))
             rough = rough + d * d
             if g > 0:
-                d = a[zl] - bx[zl, 7 + 8 * g : 15 + 8 * g, :]
+                d = a[zl] - bx[zl, 7 + 8 * g : 15 + 8 * g, IN]
             else:
                 d = jnp.where(row8 == 0, 0.0, a[zl] - pltpu.roll(a[zl], 1, 0))
             rough = rough + d * d
@@ -169,35 +172,58 @@
     def rim_copies(i):
         up, down = (r + 63) % 64, (r + 1) % 64
         left, right = (c + 3) % 4, (c + 1) % 4
+        used = slice(0, 8) if i == 0 else slice(0, 16)
+
         def copy(src, dst, d, peer):
             return pltpu.make_async_remote_copy(
                 src_ref=src, dst_ref=dst, send_sem=hs_sem.at[i, d], recv_sem=hr_sem.at[i, d],
                 device_id=peer, device_id_type=MESH,
             )
+
+        east, west = hs_col.at[i, 0], hs_col.at[i, 1]
+        low, high, own = pl.ds(0, 8), pl.ds(56, 8), pl.ds(8, TB)
         return (
-            copy(hs_row.at[i, 0], hr_row.at[i, 0], 0, (down, c)),
-            copy(hs_row.at[i, 1], hr_row.at[i, 1], 1, (up, c)),
-            copy(hs_col.at[i, 0], hr_col.at[i, 0], 2, (r, right)),
-            copy(hs_col.at[i, 1], hr_col.at[i, 1], 3, (r, left)),
+            copy(hs_row.at[i, 0, used], hr_row.at[i, 0, used], 0, (down, c)),
+            copy(hs_row.at[i, 1, used], hr_row.at[i, 1, used], 1, (up, c)),
+            copy(east, hr_col.at[i, 0, own], 2, (r, right)),
+            copy(west, hr_col.at[i, 1, own], 3, (r, left)),
+            copy(east.at[pl.ds(40, 8)], hr_col.at[i, 0, low], 4, (down, right)),
+            copy(east.at[pl.ds(0, 8)], hr_col.at[i, 0, high], 5, (up, right)),
+            copy(west.at[pl.ds(40, 8)], hr_col.at[i, 1, low], 6, (down, left)),
+            copy(west.at[pl.ds(0, 8)], hr_col.at[i, 1, high], 7, (up, left)),
         )
 
-    def rim_start(i, f):
-        for zl in range(2):
-            hs_row[i, 0, zl : zl + 1, :] = f[zl, 55:56, :]
-            hs_row[i, 1, zl : zl + 1, :] = f[zl, 8:9, :]
-        hs_col[i, 0] = jnp.where(
-            lane48 == 127, f[0, 8:56, 640:768], pltpu.roll(f[1, 8:56, 640:768], 127, 1)
-        )
-        hs_col[i, 1] = jnp.where(lane48 == 0, f[0, 8:56, 0:128], pltpu.roll(f[1, 8:56, 0:128], 1, 1))
+    def rim_start(i, planes):
+        east = west = None
+        for j, (f, zl) in enumerate(planes):
+            e = f[zl, 8:56, 768:896]
+            w = f[zl, 8:56, 128:256]
+            if j == 0:
+                east, west = e, w
+            else:
+                east = jnp.where(lane48 < 128 - 3 * j, pltpu.roll(e, 128 - 3 * j, 1), east)
+                west = jnp.where(lane48 >= 3 * j, pltpu.roll(w, 3 * j, 1), west)
+        hs_col[i, 0] = east
+        hs_col[i, 1] = west
+        for j, (f, zl) in enumerate(planes):
+            hs_row[i, 0, 3 * j : 3 * j + 3, :] = f[zl, 53:56, IN]
+            hs_row[i, 1, 3 * j : 3 * j + 3, :] = f[zl, 8:11, IN]
         for copy in rim_copies(i):
             copy.start()
 
-    def rim_wait(i, f):
+    def rim_wait(i, planes):
         for copy in rim_copies(i):
             copy.wait()
-        for zl in range(2):
-            f[zl, 7:8, :] = hr_row[i, 0, zl : zl + 1, :]
-            f[zl, 56:57, :] = hr_row[i, 1, zl : zl + 1, :]
+        east = hr_col[i, 0]
+        west = hr_col[i, 1]
+        for j, (f, zl) in enumerate(planes):
+            f[zl, 5:8, IN] = hr_row[i, 0, 3 * j : 3 * j + 3, :]
+            f[zl, 56:59, IN] = hr_row[i, 1, 3 * j : 3 * j + 3, :]
+            f[zl, :, 0:128] = east if j == 0 else pltpu.roll(east, 3 * j, 1)
+            f[zl, :, 896:1024] = west if j == 0 else pltpu.roll(west, 128 - 3 * j, 1)
+
+    source_planes = ((bx, 0), (bx, 1))
+    cell_planes = ((ix, 0), (ix, 1), (cc, 0), (cc, 1))
 
     spot_a = r % 16
     spot_b = y * 4 + c
@@ -326,13 +352,13 @@
     def _(i):
         compute(i)
 
-    pl.semaphore_wait(barrier, 77)
+    pl.semaphore_wait(barrier, 81)
 
     @pl.loop(0, WINDOW)
     def _(k):
         send(k)
 
-    rim_start(0, bx)
+    rim_start(0, source_planes)
 
     @pl.loop(0, NQ + LAG_MERGE)
     def _(it):
@@ -383,10 +409,10 @@
             for i in range(1, M):
                 inverse = inverse + m[i] * param[i]
                 heat = heat + m[i] * param[M + i]
-            ix[zl, 8:56, at] = inverse
-            cc[zl, :, at] = heat
-    rim_start(1, ix)
-    rim_wait(0, bx)
+            ix[zl, 8:56, 128 + 128 * t : 256 + 128 * t] = inverse
+            cc[zl, 8:56, 128 + 128 * t : 256 + 128 * t] = heat
+    rim_start(1, cell_planes)
+    rim_wait(0, source_planes)
 
     param = [a[:, 0:1] for a in param]
     early = jnp.sum(sum_wait(0, 1), axis=1, keepdims=True)
@@ -401,71 +427,65 @@
     sigma = mean_c / weight + early[1:2] / norm * weight / mean_i
     per = 1.0 / sigma
 
-    def beside(i, f, zl, g):
-        w = f[zl, 8 + 8 * g : 16 + 8 * g, :]
-        above = f[zl, 7 + 8 * g : 15 + 8 * g, :]
-        below = f[zl, 9 + 8 * g : 17 + 8 * g, :]
-        lane = lanes((8, 128))
-        hl = pltpu.roll(hr_col[i, 0, 8 * g : 8 * g + 8, :], 1 + zl, 1)
-        hr = pltpu.roll(hr_col[i, 1, 8 * g : 8 * g + 8, :], 127 - zl, 1)
-        left = pltpu.roll(w, 1, 1)
-        right = pltpu.roll(w, 767, 1)
-        left = jnp.concatenate([jnp.where(lane == 0, hl, left[:, 0:128]), left[:, 128:]], axis=1)
-        right = jnp.concatenate(
-            [right[:, 0:640], jnp.where(lane == 127, hr, right[:, 640:])], axis=1
-        )
-        return w, above, below, left, right
-
-    def apply(i, f, out, out_row):
+    def shifted(f, zl, g):
+        w = f[zl, 8 * g : 8 * g + 8, :]
+        above = f[zl, 8 * g - 1 : 8 * g + 7, :] if g > 0 else pltpu.roll(w, 1, 0)
+        below = f[zl, 8 * g + 1 : 8 * g + 9, :] if g < 7 else pltpu.roll(w, 7, 0)
+        return w, above, below
+
+    def apply(f, out, groups):
         odd = jnp.zeros((8, 768), F32)
         even = jnp.zeros((8, 768), F32)
         for zl in range(2):
-            for g in range(6):
+            for g in groups:
                 at = slice(8 * g, 8 * g + 8)
-                w, above, below, left, right = beside(i, f, zl, g)
-                other = f[1 - zl, 8 + 8 * g : 16 + 8 * g, :]
-                v = cc[zl, at, :] * w
-                v = v + fz[at, :] * (w - other)
-                v = v + fu[zl, at, :] * (w - above) + fd[zl, at, :] * (w - below)
-                v = v + fl[zl, at, :] * (w - left) + fr[zl, at, :] * (w - right)
-                out[zl, out_row + 8 * g : out_row + 8 * g + 8, :] = v
-                odd = odd + w * v
-                even = even + v * v
+                w, above, below = shifted(f, zl, g)
+                face_above = fu[zl, at, :]
+                v = cc[zl, at, :] * w + fz[at, :] * (w - f[1 - zl, at, :])
+                v = v + face_above * (w - above)
+                face_below = fu[zl, 8 * g + 1 : 8 * g + 9, :] if g < 7 else pltpu.roll(face_above, 7, 0)
+                v = v + face_below * (w - below)
+                flow = fl[zl, at, :] * (w - pltpu.roll(w, 1, 1))
+                v = v + (flow - pltpu.roll(flow, 1023, 1))
+                out[zl, at, :] = v
+                if 1 <= g <= 6:
+                    w, v = w[:, IN], v[:, IN]
+                    odd = odd + w * v
+                    even = even + v * v
         return rows_of(fold(odd)), rows_of(fold(even))
 
-    rim_wait(1, ix)
+    rim_wait(1, cell_planes)
     zero, one = jnp.float32(0.0), jnp.float32(1.0)
     top = jnp.where(r == 0, zero, one)
     bottom = jnp.where(r == 63, zero, one)
     first = jnp.where(c == 0, zero, one)
     last = jnp.where(c == 3, zero, one)
-    twice = jnp.broadcast_to(2.0 * per, (8, 768))
+    twice = jnp.broadcast_to(2.0 * per, (8, 1024))
+    lane_ext = lanes((8, 1024))
+    row_ext = lax.broadcasted_iota(jnp.int32, (8, 1024), 0)
+    walls = jnp.where(lane_ext == 128, first, jnp.where(lane_ext == 896, last, one))
     for zl in range(2):
-        for g in range(6):
+        for g in range(8):
             at = slice(8 * g, 8 * g + 8)
-            w, above, below, left, right = beside(1, ix, zl, g)
+            w = ix[zl, at, :]
+            above = ix[zl, 8 * g - 1 : 8 * g + 7, :] if g > 0 else pltpu.roll(w, 1, 0)
             f = twice / (w + above)
-            fu[zl, at, :] = f * jnp.where(row8 == 0, top, one) if g == 0 else f
-            f = twice / (w + below)
-            fd[zl, at, :] = f * jnp.where(row8 == 7, bottom, one) if g == 5 else f
-            fl[zl, at, :] = twice / (w + left) * jnp.where(lane8 == 0, first, one)
-            fr[zl, at, :] = twice / (w + right) * jnp.where(lane8 == 767, last, one)
+            if g in (1, 7):
+                f = f * jnp.where(row_ext == 0, top if g == 1 else bottom, one)
+            fu[zl, at, :] = f
+            fl[zl, at, :] = twice / (w + pltpu.roll(w, 1, 1)) * walls
             if zl == 0:
-                fz[at, :] = twice / (w + ix[1, 8 + 8 * g : 16 + 8 * g, :])
+                fz[at, :] = twice / (w + ix[1, at, :])
             cc[zl, at, :] = cc[zl, at, :] * per - 1.0
 
     tile_a[1] = jnp.zeros((8, 128), F32)
-    s1, s2 = apply(0, bx, v1, 8)
-    rim_start(2, v1)
+    s1, s2 = apply(bx, v1, range(8))
     tile_a[1, 0:1, :] = s1
     tile_a[1, 1:2, :] = s2
-    rim_wait(2, v1)
-    s1, s2 = apply(2, v1, v2, 8)
-    rim_start(3, v2)
+    s1, s2 = apply(v1, v2, range(8))
     tile_a[1, 2:3, :] = s1
     tile_a[1, 3:4, :] = s2
-    rim_wait(3, v2)
-    s1, s2 = apply(3, v2, v3, 0)
+    s1, s2 = apply(v2, v3, range(1, 7))
     tile_a[1, 4:5, :] = s1
     sum_start(1, 0)
     tile_b[1] = sum_wait(1, 0)
@@ -510,7 +530,7 @@
         for g in range(6):
             at = slice(8 * g, 8 * g + 8)
             ext = slice(8 + 8 * g, 16 + 8 * g)
-            base = (bx[zl, ext, :], v1[zl, ext, :], v2[zl, ext, :], v3[zl, at, :])
+            base = [v[zl, ext, IN] for v in (bx, v1, v2, v3)]
             out = x[0] * base[0]
             for i in range(1, 3):
                 out = out + x[i] * base[i]
@@ -553,8 +573,7 @@
     vmem = pl.BlockSpec(memory_space=pltpu.VMEM)
     hbm = pl.BlockSpec(memory_space=pltpu.HBM)
     shapes = (jax.ShapeDtypeStruct((2 * M, TB, 768), F32), field, field)
-    ext = VM((2, 64, 768), F32)
-    inner = VM((2, TB, 768), F32)
+    ext = VM((2, 64, 1024), F32)
     made = pl.pallas_call(
         kernel,
         out_shape=shapes,
@@ -569,15 +588,15 @@
             VM((96, 128), F32),
             VM((128, 576), BF16),
             VM((64, TB, 128), F32), VM((64, TB, 128), F32), VM((64, TB, 128), F32),
-            ext, ext, ext, ext, inner, inner,
-            inner, inner, inner, inner, VM((TB, 768), F32),
-            VM((4, 2, 2, 768), F32), VM((4, 2, 2, 768), F32),
-            VM((4, 2, TB, 128), F32), VM((4, 2, TB, 128), F32),
+            ext, ext, ext, ext, ext, ext,
+            ext, ext, VM((64, 1024), F32),
+            VM((2, 2, 16, 768), F32), VM((2, 2, 16, 768), F32),
+            VM((2, 2, TB, 128), F32), VM((2, 2, 64, 128), F32),
             VM((3, 8, 128), F32),
             VM((2, 8, 128), F32), VM((2, 16, 8, 128), F32),
             VM((2, 8, 128), F32), VM((2, 16, 8, 128), F32),
             DMA((7,)), DMA((NQ,)), DMA, DMA((64,)), DMA, DMA((64,)),
-            DMA((4, 4)), DMA((4, 4)), DMA((2, 2)), DMA((2, 2)),
+            DMA((2, 8)), DMA((2, 8)), DMA((2, 2)), DMA((2, 2)),
         ],
         compiler_params=pltpu.CompilerParams(
             collective_id=0, has_side_effects=True, vmem_limit_bytes=48 * 2**20

time: 80.8 us -> 77.2 us (0.955)
  Pallas kernels: 80 us -> 76.4 us
    pallas_call x1, Pallas kernels: 78.6 us -> 75 us  [per_device(): pl.pallas_call(kernel, out_shape=shapes, in_specs=[hbm] * 8, out_specs=(v...]
where the time goes in v5:
time: 77.2 us; the launch traced here: 77.1 us
  Pallas kernels  76.4 us (99%)
    pallas_call x1, Pallas kernels, per_device(): pl.pallas_call(kernel, out_shape=shapes, in_specs=[hbm] * 8, out_specs=(v...  75 us

profile of v5, /device:TPU:1, one launch (start us, length us, event | category | flops | bytes accessed | tf_op | source)
XLA Modules:
  0.0 77.1 jit_solution(6519061569280360197)
XLA Ops:
  0.6 75.0 %shard_map.103 = (f32[12,48,768]{2,1,0:T(8,128)S(1)}, f32[2,48,768]{2,1,0:T(8,128)S(1)}, f32[2,48,768]{2,1,0:T(8,128)S(1)}) custom-call(f32[3,64,4096]{2,1,0:T(8,128)} %frac.1, s32[4097]{0:T(1024)} %xs_edges.1, s32[3073]{0:T(1024)} %xt_edges.1, s32[4097]{0:T(1024)} %ys_edges.1, s32[3073]{0:T(1024)} %yt_edges.1, s32[6]{0:T(128)} %table_in.1, f32[6]{0:T(128)} %capacity_in.1, ...), custom_call_target="tpu_custom_call" | custom-call | tf_op jit(solution)/shard_map/pallas_call | solution.py:577
  75.7 1.4 %shard_map.104 = (f32[12,48,768]{2,1,0:T(8,128)}, f32[2,48,768]{2,1,0:T(8,128)}, f32[2,48,768]{2,1,0:T(8,128)}) custom-call(f32[12,48,768]{2,1,0:T(8,128)S(1)} %get-tuple-element.6.refs_0_, f32[2,48,768]{2,1,0:T(8,128)S(1)} %get-tuple-element.7.refs_1_, f32[2,48,768]{2,1,0:T(8,128)S(1)} %get-tuple-element.8.refs_2_), custom_call_target="tpu_custom_call" | custom-call | tf_op jit(solution)/shard_map/pallas_call | solution.py:613

commit v6 on v5

--- a/solution.py
+++ b/solution.py
@@ -9,8 +9,8 @@
 TB = 48
 NQ = 32
 GROUP = 4
-AHEAD = 12
-WINDOW = 12
+AHEAD = 8
+WINDOW = 8
 LAG_MERGE = 16
 MESH = pl.DeviceIdType.MESH
 F32 = jnp.float32
@@ -31,7 +31,8 @@
 
 def offsets(k, c):
     g, s = k // 8, k % 2
-    dz = jnp.where(s == 0, 4 - g, jnp.where(g == 0, 0, 4 + g))
+    far = (g + 1) % 4
+    dz = jnp.where(s == 0, 4 - far, jnp.where(far == 0, 0, 4 + far))
     return (k // 2 + c) % 4, dz
 
 
@@ -53,6 +54,29 @@
     y, z = chip // 8, chip % 8
     half = c % 2
 
+    barrier = pltpu.get_barrier_semaphore()
+
+    def greet(row, col):
+        pl.semaphore_signal(barrier, inc=1, device_id=(row, col), device_id_type=MESH)
+
+    @pl.loop(0, 63)
+    def _(j):
+        j = (j + 31) % 63 + 1
+        greet(16 * y + (r + j // 4) % 16, (c + j % 4) % 4)
+
+    @pl.loop(0, 9)
+    def _(j):
+        greet((r + 16 * (1 + j // 3)) % 64, (c + 1 + j % 3) % 4)
+
+    @pl.loop(1, 4)
+    def _(j):
+        greet((r + 16 * j) % 64, c)
+
+    for side in (1, 63):
+        greet((r + side) % 64, c)
+        greet((r + side) % 64, (c + 1) % 4)
+        greet((r + side) % 64, (c + 3) % 4)
+
     lines = ((xs_edges, xs_line), (xt_edges, xt_line), (ys_edges, ys_line), (yt_edges, yt_line))
     early_copies = [pltpu.make_async_copy(a, b, esem.at[i]) for i, (a, b) in enumerate(lines)]
     early_copies.append(pltpu.make_async_copy(b_ref, bx.at[:, 8:56, IN], esem.at[4]))
@@ -71,28 +95,6 @@
     @pl.loop(0, NQ)
     def _(k):
         fetch(k).start()
-
-    barrier = pltpu.get_barrier_semaphore()
-
-    def greet(row, col):
-        pl.semaphore_signal(barrier, inc=1, device_id=(row, col), device_id_type=MESH)
-
-    @pl.loop(1, 64)
-    def _(j):
-        greet(16 * y + (r + j // 4) % 16, (c + j % 4) % 4)
-
-    @pl.loop(1, 4)
-    def _(j):
-        greet((r + 16 * j) % 64, c)
-
-    for side in (1, 63):
-        greet((r + side) % 64, c)
-        greet((r + side) % 64, (c + 1) % 4)
-        greet((r + side) % 64, (c + 3) % 4)
-
-    @pl.loop(0, 9)
-    def _(j):
-        greet((r + 16 * (1 + j // 3)) % 64, (c + 1 + j % 3) % 4)
 
     for i, (line, rows) in enumerate(
         ((xs_line, xs_rows), (xt_line, xt_rows), (ys_line, ys_rows), (yt_line, yt_rows))
@@ -242,9 +244,9 @@
         )
 
     def sum_start(i, stage):
-        @pl.loop(1, 16)
+        @pl.loop(0, 15)
         def _(j):
-            sum_copy(i, stage, j).start()
+            sum_copy(i, stage, (j + 7) % 15 + 1).start()
 
     def sum_wait(i, stage):
         got = got_a if stage == 0 else got_b
@@ -263,13 +265,13 @@
         wh, wl = split(pair_weights(ys_rows, yt_rows, ((y + dy) % 4) * 8 + (z + dz) % 8))
         return jnp.concatenate([wh, wh, wl], axis=1)
 
-    def compute(i):
+    def compute(i, early):
         steps = [GROUP * i + j for j in range(GROUP)]
         for k in steps:
             fetch(k).wait()
         wy = [weights_y(k) for k in steps]
         cells = [fbuf[k] for k in steps]
-        for f in cells:
+        for f in cells if early else ():
             for p in range(3):
                 acc[p] = acc[p] + jnp.sum(f[p].reshape(8, 8, 128), axis=0)
         outs = []
@@ -350,9 +352,16 @@
 
     @pl.loop(0, AHEAD // GROUP)
     def _(i):
-        compute(i)
+        compute(i, True)
+
+    hf = half.astype(F32)
+    for p in range(3):
+        v = rows_of(acc[p])
+        tile_a[0, 2 + p : 3 + p, :] = v * (1.0 - hf)
+        tile_a[0, 5 + p : 6 + p, :] = v * hf
 
     pl.semaphore_wait(barrier, 81)
+    sum_start(0, 0)
 
     @pl.loop(0, WINDOW)
     def _(k):
@@ -364,16 +373,7 @@
     def _(it):
         @pl.when(jnp.logical_and(it < NQ - AHEAD, it % GROUP == 0))
         def _():
-            compute((it + AHEAD) // GROUP)
-
-        @pl.when(it == NQ - AHEAD)
-        def _():
-            hf = half.astype(F32)
-            for p in range(3):
-                v = rows_of(acc[p])
-                tile_a[0, 2 + p : 3 + p, :] = v * (1.0 - hf)
-                tile_a[0, 5 + p : 6 + p, :] = v * hf
-            sum_start(0, 0)
+            compute((it + AHEAD) // GROUP, False)
 
         @pl.when(it < NQ)
         def _():
@@ -383,7 +383,7 @@
         def _():
             send(it + WINDOW)
 
-        @pl.when(it == NQ - AHEAD + 8)
+        @pl.when(it == 8)
         def _():
             tile_b[0] = sum_wait(0, 0)
             sum_start(0, 1)

time: 77.2 us -> 76 us (0.984)
  Pallas kernels: 76.4 us -> 75.3 us
    pallas_call x1, Pallas kernels: 75 us -> 73.9 us  [per_device(): pl.pallas_call(kernel, out_shape=shapes, in_specs=[hbm] * 8, out_specs=(v...]
where the time goes in v6:
time: 76 us; the launch traced here: 75.9 us
  Pallas kernels  75.3 us (99%)
    pallas_call x1, Pallas kernels, per_device(): pl.pallas_call(kernel, out_shape=shapes, in_specs=[hbm] * 8, out_specs=(v...  73.9 us

profile of v6, /device:TPU:1, one launch (start us, length us, event | category | flops | bytes accessed | tf_op | source)
XLA Modules:
  0.0 75.9 jit_solution(2861943390262986413)
XLA Ops:
  0.6 73.9 %shard_map.103 = (f32[12,48,768]{2,1,0:T(8,128)S(1)}, f32[2,48,768]{2,1,0:T(8,128)S(1)}, f32[2,48,768]{2,1,0:T(8,128)S(1)}) custom-call(f32[3,64,4096]{2,1,0:T(8,128)} %frac.1, s32[4097]{0:T(1024)} %xs_edges.1, s32[3073]{0:T(1024)} %xt_edges.1, s32[4097]{0:T(1024)} %ys_edges.1, s32[3073]{0:T(1024)} %yt_edges.1, s32[6]{0:T(128)} %table_in.1, f32[6]{0:T(128)} %capacity_in.1, ...), custom_call_target="tpu_custom_call" | custom-call | tf_op jit(solution)/shard_map/pallas_call | solution.py:577
  74.5 1.4 %shard_map.104 = (f32[12,48,768]{2,1,0:T(8,128)}, f32[2,48,768]{2,1,0:T(8,128)}, f32[2,48,768]{2,1,0:T(8,128)}) custom-call(f32[12,48,768]{2,1,0:T(8,128)S(1)} %get-tuple-element.6.refs_0_, f32[2,48,768]{2,1,0:T(8,128)S(1)} %get-tuple-element.7.refs_1_, f32[2,48,768]{2,1,0:T(8,128)S(1)} %get-tuple-element.8.refs_2_), custom_call_target="tpu_custom_call" | custom-call | tf_op jit(solution)/shard_map/pallas_call | solution.py:613
